TPU v7x, 32 devices: a whole 2x2x4 slice. The times are simulated.
32 devices in a mesh: groups: 2 (over y), snd: 4 (over z), win: 2 (over x), pt: 2 (over core).
Axes of the slice: x: 2, y: 2, z: 4, core: 2. Of those that a mesh axis runs over, the one named last changes fastest.
Arguments:
- flux_state: float32 [4, 256, 16, 128], P(('groups', 'win'), 'snd', 'pt'), parts along dimension 0, may hold values from -6 to 6
- prior_precision: float32 [4, 256, 128], P(('groups', 'win'), 'snd'), parts along dimension 0, may hold values from 0.05 to 0.5
- footprint: bfloat16 [64, 32, 128, 128], P(('groups', 'snd'), 'win'), parts along dimension 0, may hold values from -0.125 to 0.125
- tile_ids: int32 [64, 32], P(('groups', 'snd'), 'win'), parts along dimension 0, may hold values from 0 to 255, as said below
- observed: float32 [64, 128], P(('groups', 'snd')), parts along dimension 0, may hold values from -6 to 6
- obs_weight: float32 [64, 128], P(('groups', 'snd')), parts along dimension 0, may hold values from 0.1 to 1
Outputs:
- gradient: float32 [4, 256, 16, 128], P(('groups', 'win'), 'snd', 'pt'), parts along dimension 0
There are 2 independent parts, one for each index of `groups`. A program takes and returns all parts, laid end to end along the dimension named above; each array names one. Nothing has to cross between parts.
Inputs may be any that keep to these rules, and one draw needn't show every extreme that they name: `tile_ids`: column block w (entries w * 16 to w * 16 + 15) belongs to window w. Within the 8 rows and 16 columns of one window held by one device the entries are distinct, and at most 64 of them lie among the 64 tiles t with the same t // 64; in every window one such range is named exactly 64 times by every device.
All inputs are finite; a program needn't handle non-finite values.
Results may differ from a plain program's by a relative error of at most 0.0029.
Values may be sent and summed in bfloat16 or wider, within the bound.
No kernel may reach another device: no remote copies, remote signals or barrier semaphores. Data moves between devices by JAX's collectives and lax.ppermute only.
A program may use at most 64 MiB of HBM per device.

v0:
```python
import jax
import jax.numpy as jnp
from jax import lax
from jax.sharding import PartitionSpec as P


def body(flux_state, prior_precision, footprint, tile_ids, observed, obs_weight):
    flux_local = flux_state[0]
    own_tiles, half_points, tile_cells = flux_local.shape
    blocks, tile_depth = tile_ids.shape
    ref_count = blocks * tile_depth
    flat_ids = tile_ids.reshape(ref_count)
    rounded = flux_local.astype(jnp.bfloat16)
    window_flux = lax.all_gather(rounded, "snd", axis=0, tiled=True)
    gathered = window_flux[flat_ids].reshape(blocks, tile_depth, half_points, tile_cells)
    window_part = jnp.einsum(
        "bksf,bkpf->bps", footprint, gathered, preferred_element_type=jnp.float32
    )
    modeled = lax.psum(window_part, "win")
    residual = (obs_weight[:, None, :] * (modeled - observed[:, None, :])).astype(jnp.bfloat16)
    contrib = jnp.einsum("bps,bksf->bkpf", residual, footprint, preferred_element_type=jnp.float32)
    contrib = contrib.reshape(ref_count, half_points * tile_cells)
    window_tiles = window_flux.shape[0]
    dense_terms = (
        jnp.zeros((window_tiles, half_points * tile_cells), jnp.float32).at[flat_ids].add(contrib)
    )
    summed = lax.psum_scatter(
        dense_terms.reshape(own_tiles * lax.axis_size("snd"), half_points, tile_cells),
        "snd",
        scatter_dimension=0,
        tiled=True,
    )
    gradient = summed + prior_precision[0][:, None, :] * flux_local
    return gradient[None]


def solution(mesh):
    placed = (
        P(("groups", "win"), "snd", "pt", None),
        P(("groups", "win"), "snd", None),
        P(("groups", "snd"), "win", None, None),
        P(("groups", "snd"), "win"),
        P(("groups", "snd"), None),
        P(("groups", "snd"), None),
    )
    return jax.shard_map(
        body,
        mesh=mesh,
        in_specs=placed,
        out_specs=P(("groups", "win"), "snd", "pt", None),
        check_vma=False,
    )
```

profile of v0, /device:TPU:0, one launch (start us, length us, event | category | flops | bytes accessed | tf_op | source)
XLA Modules:
  0.0 80.9 jit_solution(8460589797217001848)
XLA Ops:
  6.5 0.0 copy-start.3
  6.5 0.0 copy-start.2
  6.5 0.0 reduce-scatter.2.cloned.1.call-start
  6.5 0.8 reshape.43
  7.3 1.0 %bitcast_convert_fusion = bf16[64,8,128]{2,1,0:T(8,128)(2,1)S(1)} fusion(f32[1,64,8,128]{3,2,1,0:T(8,128)} %param.6), kind=kLoop, calls=%fused_computation.8 | loop fusion | flops 65536 | bytes 393216 | tf_op jit(solution)/shard_map/convert_element_type | solution.py:13
  8.3 17.4 %all_gather.3 = bf16[256,8,128]{2,1,0:T(8,128)(2,1)S(1)} all-gather(bf16[64,8,128]{2,1,0:T(8,128)(2,1)S(1)} %bitcast_convert_fusion), channel_id=1, replica_groups=mesh['groups'=2,'snd'=4,'win'=2,'pt'=2] {'snd'}, dimensions={0}, use_global_device_ids=true | all-gather | bytes 655360 | tf_op jit(solution)/shard_map/all_gather | solution.py:14
  25.7 0.7 gather_fusion
  26.4 3.4 %convolution_bitcast_fusion = f32[8,8,128]{2,1,0:T(8,128)S(1)} fusion(bf16[8,16,8,128]{3,2,1,0:T(8,128)(2,1)S(1)} %bitcast.35, bf16[8,16,128,128]{3,2,1,0:T(8,128)(2,1)} %param.8), kind=kOutput, calls=%fused_computation.2 | convolution fusion | flops 33554432 | bytes 4489216 | tf_op jit(solution)/shard_map/bksf,bkpf->bps/dot_general | solution.py:16
  29.7 8.4 %psum.7 = f32[8,8,128]{2,1,0:T(8,128)S(1)} all-reduce(f32[8,8,128]{2,1,0:T(8,128)S(1)} %convolution_bitcast_fusion), channel_id=1, replica_groups=mesh['groups'=2,'snd'=4,'win'=2,'pt'=2] {'win'}, use_global_device_ids=true, to_apply=%region_0.0 | all-reduce | flops 8192 | bytes 65536 | tf_op jit(solution)/shard_map/psum | solution.py:19
  38.1 0.0 copy-done.3
  38.1 0.0 copy-done.2
  38.1 0.0 copy-start
  38.1 0.0 copy-start.1
  38.1 2.9 %fusion.7 = f32[8,8,16,128]{3,1,2,0:T(8,128)S(1)} fusion(bf16[8,16,128,128]{3,2,1,0:T(8,128)(2,1)} %param.8, f32[8,8,128]{2,1,0:T(8,128)S(1)} %psum.7, f32[8,128]{1,0:T(8,128)S(1)} %copy-done.2, f32[8,128]{1,0:T(8,128)S(1)} %copy-done.3), kind=kOutput, calls=%fused_computation.13 | convolution fusion | flops 33579008 | bytes 4759552 | tf_op jit(solution)/shard_map/bps,bksf->bkpf/dot_general | solution.py:21
  41.0 2.0 %scatter_custom_fusion = f32[256,1024]{1,0:T(8,128)S(1)} fusion(s32[128]{0:T(128)S(1)} %fusion.11, f32[16,8,8,128]{3,2,1,0:T(8,128)S(1)} %bitcast.34, f32[]{:T(128)} %constant.0.clone.1), kind=kCustom, calls=%fused_computation.3 | custom fusion | flops 131072 | bytes 1572868 | tf_op jit(solution)/shard_map/scatter-add | solution.py:25
  43.0 1.2 %copy.10 = f32[32,8,8,128]{3,2,1,0:T(8,128)} copy(f32[32,8,8,128]{3,1,2,0:T(8,128)S(1)} %bitcast.33) | data formatting | bytes 2097152
  44.2 0.0 reduce-scatter.2.cloned.1.call-update
  44.2 28.1 %reduce-scatter.2.cloned.1.call-done = f32[64,8,128]{2,1,0:T(8,128)} async-done(((f32[256,8,128]{2,1,0:T(8,128)}), f32[64,8,128]{2,1,0:T(8,128)}) %reduce-scatter.2.cloned.1.call-update) | async-done | bytes 262160 | tf_op jit(solution)/shard_map/reduce_scatter | solution.py:27
  72.3 0.0 copy-done
  72.3 0.0 copy-done.1
  72.3 1.7 %fusion.5 = f32[1,64,8,128]{3,2,1,0:T(8,128)} fusion(f32[64,8,128]{2,1,0:T(8,128)} %reduce-scatter.2.cloned.1.call-done, f32[1,64,8,128]{3,2,1,0:T(8,128)S(1)} %copy-done, f32[64,128]{1,0:T(8,128)S(1)} %bitcast.36), kind=kLoop, calls=%fused_computation.10 | loop fusion | flops 131072 | bytes 819200 | tf_op jit(solution)/shard_map/broadcast_in_dim | solution.py:34
  (2 shorter events, 0.0 us)
Async XLA Ops:
  6.5 31.6 %copy-start.3 = (f32[8,128]{1,0:T(8,128)S(1)}, f32[8,128]{1,0:T(8,128)}, u32[]{:S(2)}) copy-start(f32[8,128]{1,0:T(8,128)} %param.11) | copy-start | bytes 12292
  6.5 31.6 %copy-start.2 = (f32[8,128]{1,0:T(8,128)S(1)}, f32[8,128]{1,0:T(8,128)}, u32[]{:S(2)}) copy-start(f32[8,128]{1,0:T(8,128)} %param.10) | copy-start | bytes 12292
  6.5 65.8 %reduce-scatter.2.cloned.1.call-start = ((), (), s32[]{:S(2)}) async-start(), calls=%async_computation.1 | async-start | bytes 1310720 | tf_op jit(solution)/shard_map/reduce_scatter | solution.py:27
  38.1 34.2 %copy-start = (f32[1,64,8,128]{3,2,1,0:T(8,128)S(1)}, f32[1,64,8,128]{3,2,1,0:T(8,128)}, u32[]{:S(2)}) copy-start(f32[1,64,8,128]{3,2,1,0:T(8,128)} %param.6) | copy-start | bytes 786436
  38.1 34.2 %copy-start.1 = (f32[1,64,128]{2,1,0:T(8,128)S(1)}, f32[1,64,128]{2,1,0:T(8,128)}, u32[]{:S(2)}) copy-start(f32[1,64,128]{2,1,0:T(8,128)} %param.7) | copy-start | bytes 98308
Sparse Core Ops, SparseCore 0:
  44.3 27.9 reduce-scatter.1
where the time goes:
time: 81.1 us; the launch traced here: 80.9 us
  waiting for transfers between devices  28.2 us (35%)
  blocking collectives  25.7 us (32%)
  between operations  13.4 us (17%)
  matrix products  6.24 us (8%)
  other arithmetic  4.64 us (6%)
  local copies, waits for them, and re-layouts  2.69 us (3%)
    reduce_scatter x1, waiting for transfers between devices, body(): lax.psum_scatter(dense_terms.reshape(own_tiles * lax.axis_size('snd'), ha...  28.1 us
    all_gather x1, blocking collectives, body(): window_flux = lax.all_gather(rounded, 'snd', axis=0, tiled=True)  17.4 us
    psum x1, blocking collectives, body(): modeled = lax.psum(window_part, 'win')  8.35 us
    dot_general x1, matrix products, body(): jnp.einsum('bksf,bkpf->bps', footprint, gathered, preferred_element_type=...  3.36 us
    dot_general x1, matrix products, body(): jnp.einsum('bps,bksf->bkpf', residual, footprint, preferred_element_type=...  2.88 us
    scatter-add x1, other arithmetic, body(): jnp.zeros((window_tiles, half_points * tile_cells), jnp.float32)  1.96 us
    broadcast_in_dim x1, other arithmetic, body(): return gradient[None]  1.69 us
  transfers between devices with their start and end apart: 1, of which 1 were waited for; matrix products, arithmetic and copies ran while one was open for 0% of the time, Pallas kernels for 0%

commit v1 on v0

v1 whole, which is shorter than its diff:
```python
import functools

import jax
import jax.numpy as jnp
from jax import lax
from jax.experimental import pallas as pl
from jax.experimental.pallas import tpu as pltpu
from jax.sharding import PartitionSpec as P

BF16 = jnp.bfloat16
F32 = jnp.float32
VMEM = pl.BlockSpec(memory_space=pltpu.VMEM)
SMEM = pl.BlockSpec(memory_space=pltpu.SMEM)
PARAMS = pltpu.CompilerParams(vmem_limit_bytes=40 << 20)


def partner_pairs(n, step):
    if n & (n - 1) == 0:
        return [(i, i ^ step) for i in range(n)]
    return [(i, (i + step) % n) for i in range(n)]


def slot_of(n, me, owner):
    if n & (n - 1) == 0:
        return me ^ owner
    return lax.rem(me - owner + n, n)


def send_slot_of(n, me, owner):
    if n & (n - 1) == 0:
        return me ^ owner
    return lax.rem(owner - me + n, n)


def modeled_kernel(n, ids_ref, *refs):
    shards = refs[:n]
    foot_ref, out_ref, all_ref, lhs_ref = refs[n:]
    tiles = shards[0].shape[0]
    blocks, depth = ids_ref.shape
    cells = foot_ref.shape[3]
    me = lax.axis_index("snd")
    for slot in range(n):
        all_ref[pl.ds(slot * tiles, tiles)] = shards[slot][...]
    for b in range(blocks):
        for k in range(depth):
            t = ids_ref[b, k]
            owner = lax.div(t, tiles)
            at = slot_of(n, me, owner) * tiles + (t - owner * tiles)
            lhs_ref[b, :, pl.ds(k * cells, cells)] = all_ref[at]
        rhs = jnp.concatenate([foot_ref[b, k] for k in range(depth)], axis=1)
        out_ref[b] = lax.dot_general(
            lhs_ref[b], rhs, (((1,), (1,)), ((), ())), preferred_element_type=F32
        )


def gradient_kernel(n, ids_ref, mine_ref, other_ref, obs_ref, weight_ref, foot_ref, *refs):
    outs, dense_ref = refs[:n], refs[n]
    tiles = outs[0].shape[0]
    blocks, depth = ids_ref.shape
    cells = foot_ref.shape[3]
    me = lax.axis_index("snd")
    dense_ref[...] = jnp.zeros_like(dense_ref)
    for b in range(blocks):
        modeled = mine_ref[b] + other_ref[b]
        resid = (weight_ref[pl.ds(b, 1), :] * (modeled - obs_ref[pl.ds(b, 1), :])).astype(BF16)
        rhs = jnp.concatenate([foot_ref[b, k] for k in range(depth)], axis=1)
        terms = jnp.dot(resid, rhs, preferred_element_type=F32)
        for k in range(depth):
            t = ids_ref[b, k]
            owner = lax.div(t, tiles)
            at = send_slot_of(n, me, owner) * tiles + (t - owner * tiles)
            dense_ref[at] = terms[:, k * cells : (k + 1) * cells]
    for slot in range(n):
        outs[slot][...] = dense_ref[pl.ds(slot * tiles, tiles)].astype(outs[slot].dtype)


def final_kernel(n, flux_ref, prior_ref, own_ref, *refs):
    arrived, out_ref = refs[: n - 1], refs[n - 1]
    total = own_ref[...] + prior_ref[...][:, None, :] * flux_ref[...]
    for a in arrived:
        total += a[...].astype(F32)
    out_ref[...] = total


def body(flux_state, prior_precision, footprint, tile_ids, observed, obs_weight):
    n = lax.axis_size("snd")
    windows = lax.axis_size("win")
    flux = flux_state[0]
    tiles, points, cells = flux.shape
    blocks, depth, soundings, _ = footprint.shape
    rounded = flux.astype(BF16)
    shards = [rounded] + [lax.ppermute(rounded, "snd", partner_pairs(n, s)) for s in range(1, n)]

    mine = pl.pallas_call(
        functools.partial(modeled_kernel, n),
        out_shape=jax.ShapeDtypeStruct((blocks, points, soundings), F32),
        in_specs=[SMEM] + [VMEM] * (n + 1),
        out_specs=VMEM,
        scratch_shapes=[
            pltpu.VMEM((n * tiles, points, cells), BF16),
            pltpu.VMEM((blocks, points, depth * cells), BF16),
        ],
        compiler_params=PARAMS,
        name="modeled",
    )(tile_ids, *shards, footprint)

    if windows == 2:
        other = lax.ppermute(mine, "win", [(0, 1), (1, 0)])
    else:
        other = lax.psum(mine, "win") - mine
    grads = pl.pallas_call(
        functools.partial(gradient_kernel, n),
        out_shape=[jax.ShapeDtypeStruct((tiles, points, cells), F32)]
        + [jax.ShapeDtypeStruct((tiles, points, cells), BF16)] * (n - 1),
        in_specs=[SMEM] + [VMEM] * 5,
        out_specs=[VMEM] * n,
        scratch_shapes=[pltpu.VMEM((n * tiles, points, cells), F32)],
        compiler_params=PARAMS,
        name="terms",
    )(tile_ids, mine, other, observed, obs_weight, footprint)
    arrived = [lax.ppermute(grads[s], "snd", partner_pairs(n, s)) for s in range(1, n)]
    gradient = pl.pallas_call(
        functools.partial(final_kernel, n),
        out_shape=jax.ShapeDtypeStruct((tiles, points, cells), F32),
        in_specs=[VMEM] * (n + 2),
        out_specs=VMEM,
        compiler_params=PARAMS,
        name="total",
    )(flux, prior_precision[0], grads[0], *arrived)
    return gradient[None]


def solution(mesh):
    placed = (
        P(("groups", "win"), "snd", "pt", None),
        P(("groups", "win"), "snd", None),
        P(("groups", "snd"), "win", None, None),
        P(("groups", "snd"), "win"),
        P(("groups", "snd"), None),
        P(("groups", "snd"), None),
    )
    return jax.shard_map(
        body,
        mesh=mesh,
        in_specs=placed,
        out_specs=P(("groups", "win"), "snd", "pt", None),
        check_vma=False,
    )
```

time: 81.1 us -> 39.8 us (0.49)
  blocking collectives: 25.7 us -> 0 us
  between operations: 13.4 us -> 0.04 us
  starting transfers between devices: 0.01 us -> 11.7 us
  waiting for transfers between devices: 28.2 us -> 19.9 us
  matrix products: 6.24 us -> 0 us
  Pallas kernels: 0 us -> 3.99 us
  other arithmetic: 4.64 us -> 1.03 us
    reduce_scatter x1 -> x0, waiting for transfers between devices: 28.1 us -> none  [body(): lax.psum_scatter(dense_terms.reshape(own_tiles * lax.axis_size('snd'), ha...]
    ppermute x0 -> x7, waiting for transfers between devices: none -> 19.9 us  [the longest x3 10.4 us: body(): lax.ppermute(rounded, 'snd', partner_pairs(n, s))]
    all_gather x1 -> x0, blocking collectives: 17.4 us -> none  [body(): window_flux = lax.all_gather(rounded, 'snd', axis=0, tiled=True)]
    ppermute x0 -> x7, starting transfers between devices: none -> 11.7 us  [the longest x3 5.76 us: body(): lax.ppermute(rounded, 'snd', partner_pairs(n, s))]
    psum x1 -> x0, blocking collectives: 8.35 us -> none  [body(): modeled = lax.psum(window_part, 'win')]
    dot_general x2 -> x0, matrix products: 6.24 us -> none  [the longest x1 3.36 us: body(): jnp.einsum('bksf,bkpf->bps', footprint, gathered, preferred_element_type=...]
    pallas_call x0 -> x3, Pallas kernels: none -> 3.99 us  [the longest x1 1.81 us: body(): pl.pallas_call(functools.partial(modeled_kernel, n), out_shape=jax.ShapeD...]
    scatter-add x1 -> x0, other arithmetic: 1.96 us -> none  [body(): jnp.zeros((window_tiles, half_points * tile_cells), jnp.float32)]
  transfers between devices with their start and end apart: 1 -> 7, of which waited for: 1 -> 5; matrix products, arithmetic and copies ran while one was open for 0% -> 0% of each run, Pallas kernels for 0% -> 0%
where the time goes in v1:
time: 39.8 us; the launch traced here: 39.6 us
  waiting for transfers between devices  19.9 us (50%)
  starting transfers between devices  11.7 us (29%)
  Pallas kernels  3.99 us (10%)
  local copies, waits for them, and re-layouts  2.89 us (7%)
  other arithmetic  1.03 us (3%)
    ppermute x3, waiting for transfers between devices, body(): lax.ppermute(rounded, 'snd', partner_pairs(n, s))  10.4 us
    ppermute x3, waiting for transfers between devices, body(): lax.ppermute(grads[s], 'snd', partner_pairs(n, s))  7.06 us
    ppermute x3, starting transfers between devices, body(): lax.ppermute(rounded, 'snd', partner_pairs(n, s))  5.76 us
    ppermute x3, starting transfers between devices, body(): lax.ppermute(grads[s], 'snd', partner_pairs(n, s))  4.44 us
    unnamed x14, local copies, waits for them, and re-layouts  2.89 us
    ppermute x1, waiting for transfers between devices, body(): other = lax.ppermute(mine, 'win', [(0, 1), (1, 0)])  2.42 us
    pallas_call x1, Pallas kernels, body(): pl.pallas_call(functools.partial(modeled_kernel, n), out_shape=jax.ShapeD...  1.81 us
    ppermute x1, starting transfers between devices, body(): other = lax.ppermute(mine, 'win', [(0, 1), (1, 0)])  1.51 us
  transfers between devices with their start and end apart: 7, of which 5 were waited for; matrix products, arithmetic and copies ran while one was open for 0% of the time, Pallas kernels for 0%

profile of v1, /device:TPU:0, one launch (start us, length us, event | category | flops | bytes accessed | tf_op | source)
XLA Modules:
  0.0 39.6 jit_solution(11571572988203203053)
XLA Ops:
  0.0 1.0 %bitcast_convert_fusion.refs_0_ = bf16[64,8,128]{2,1,0:T(8,128)(2,1)S(1)} fusion(f32[1,64,8,128]{3,2,1,0:T(8,128)} %param.6), kind=kLoop, calls=%fused_computation | loop fusion | flops 65536 | bytes 393216 | tf_op jit(solution)/shard_map/convert_element_type | solution.py:91
  1.0 5.1 %collective-permute-start.2 = (bf16[64,8,128]{2,1,0:T(8,128)(2,1)S(1)}, bf16[64,8,128]{2,1,0:T(8,128)(2,1)S(1)}, u32[]{:S(2)}, u32[]{:S(2)}) collective-permute-start(bf16[64,8,128]{2,1,0:T(8,128)(2,1)S(1)} %bitcast_convert_fusion.refs_0_), channel_id=1, source_target_pairs={{0,12},{4,8},{8,4},{12,0},{1,13},{5,9},{9,5},{13,1},{2,14},{6,10},... | collective-permute-start | bytes 393224 | tf_op jit(solution)/shard_map/ppermute | solution.py:92
  6.2 0.0 collective-permute-start.1
  6.2 0.6 %collective-permute-start = (bf16[64,8,128]{2,1,0:T(8,128)(2,1)S(1)}, bf16[64,8,128]{2,1,0:T(8,128)(2,1)S(1)}, u32[]{:S(2)}, u32[]{:S(2)}) collective-permute-start(bf16[64,8,128]{2,1,0:T(8,128)(2,1)S(1)} %bitcast_convert_fusion.refs_0_), channel_id=1, source_target_pairs={{0,4},{4,0},{8,12},{12,8},{1,5},{5,1},{9,13},{13,9},{2,6},{6,2},{1... | collective-permute-start | bytes 393224 | tf_op jit(solution)/shard_map/ppermute | solution.py:92
  6.8 3.8 %collective-permute-done.2.refs_3_ = bf16[64,8,128]{2,1,0:T(8,128)(2,1)S(1)} collective-permute-done((bf16[64,8,128]{2,1,0:T(8,128)(2,1)S(1)}, bf16[64,8,128]{2,1,0:T(8,128)(2,1)S(1)}, u32[]{:S(2)}, u32[]{:S(2)}) %collective-permute-start.2) | collective-permute-done | bytes 131104 | tf_op jit(solution)/shard_map/ppermute | solution.py:92
  10.6 6.6 %collective-permute-done.1.refs_2_ = bf16[64,8,128]{2,1,0:T(8,128)(2,1)S(1)} collective-permute-done((bf16[64,8,128]{2,1,0:T(8,128)(2,1)S(1)}, bf16[64,8,128]{2,1,0:T(8,128)(2,1)S(1)}, u32[]{:S(2)}, u32[]{:S(2)}) %collective-permute-start.1) | collective-permute-done | bytes 131104 | tf_op jit(solution)/shard_map/ppermute | solution.py:92
  17.2 0.0 collective-permute-done.refs_1_
  17.2 2.2 %copy-done = bf16[8,16,128,128]{3,2,1,0:T(8,128)(2,1)S(1)} copy-done((bf16[8,16,128,128]{3,2,1,0:T(8,128)(2,1)S(1)}, bf16[8,16,128,128]{3,2,1,0:T(8,128)(2,1)}, u32[]{:S(2)}) %copy-start) | copy-done | bytes 4194328
  19.4 0.7 %copy-done.4 = s32[8,16]{1,0:T(8,128)S(1)} copy-done((s32[8,16]{1,0:T(8,128)S(1)}, s32[8,16]{1,0:T(8,128)}, u32[]{:S(2)}) %copy-start.4) | copy-done | bytes 536
  20.1 1.8 %modeled.1.mine_ref = f32[8,8,128]{2,1,0:T(8,128)S(1)} custom-call(s32[8,16]{1,0:T(8,128)S(1)} %copy-done.4, bf16[64,8,128]{2,1,0:T(8,128)(2,1)S(1)} %bitcast_convert_fusion.refs_0_, bf16[64,8,128]{2,1,0:T(8,128)(2,1)S(1)} %collective-permute-done.refs_1_, bf16[64,8,128]{2,1,0:T(8,128)(2,1)S(1)} %collective-permute-done.1.refs_2_, ...), custom_call_target="tpu_custom_call" | custom-call | tf_op jit(solution)/shard_map/modeled/pallas_call | solution.py:94
  21.9 1.5 %collective-permute-start.3 = (f32[8,8,128]{2,1,0:T(8,128)S(1)}, f32[8,8,128]{2,1,0:T(8,128)S(1)}, u32[]{:S(2)}, u32[]{:S(2)}) collective-permute-start(f32[8,8,128]{2,1,0:T(8,128)S(1)} %modeled.1.mine_ref), channel_id=1, source_target_pairs={{0,2},{2,0},{1,3},{3,1},{4,6},{6,4},{5,7},{7,5},{8,10},{10,8},{9,1... | collective-permute-start | bytes 98312 | tf_op jit(solution)/shard_map/ppermute | solution.py:108
  23.4 2.4 %collective-permute-done.3.other_ref = f32[8,8,128]{2,1,0:T(8,128)S(1)} collective-permute-done((f32[8,8,128]{2,1,0:T(8,128)S(1)}, f32[8,8,128]{2,1,0:T(8,128)S(1)}, u32[]{:S(2)}, u32[]{:S(2)}) %collective-permute-start.3) | collective-permute-done | bytes 32800 | tf_op jit(solution)/shard_map/ppermute | solution.py:108
  25.9 0.0 copy-done.6
  25.9 0.0 copy-done.5
  25.9 0.0 copy-done.1
  25.9 1.4 %terms.1 = (f32[64,8,128]{2,1,0:T(8,128)S(1)}, bf16[64,8,128]{2,1,0:T(8,128)(2,1)S(1)}, bf16[64,8,128]{2,1,0:T(8,128)(2,1)S(1)}, bf16[64,8,128]{2,1,0:T(8,128)(2,1)S(1)}) custom-call(s32[8,16]{1,0:T(8,128)S(1)} %copy-done.4, f32[8,8,128]{2,1,0:T(8,128)S(1)} %modeled.1.mine_ref, f32[8,8,128]{2,1,0:T(8,128)S(1)} %collective-permute-done.3.other_ref, ...), custom_call_target="tpu_custom_call" | custom-call | tf_op jit(solution)/shard_map/terms/pallas_call | solution.py:111
  27.2 0.1 collective-permute-start.4
  27.3 3.0 %collective-permute-start.5 = (bf16[64,8,128]{2,1,0:T(8,128)(2,1)S(1)}, bf16[64,8,128]{2,1,0:T(8,128)(2,1)S(1)}, u32[]{:S(2)}, u32[]{:S(2)}) collective-permute-start(bf16[64,8,128]{2,1,0:T(8,128)(2,1)S(1)} %get-tuple-element.11), channel_id=1, source_target_pairs={{0,8},{4,12},{8,0},{12,4},{1,9},{5,13},{9,1},{13,5},{2,10},{6,14},... | collective-permute-start | bytes 393224 | tf_op jit(solution)/shard_map/ppermute | solution.py:121
  30.4 1.3 %collective-permute-start.6 = (bf16[64,8,128]{2,1,0:T(8,128)(2,1)S(1)}, bf16[64,8,128]{2,1,0:T(8,128)(2,1)S(1)}, u32[]{:S(2)}, u32[]{:S(2)}) collective-permute-start(bf16[64,8,128]{2,1,0:T(8,128)(2,1)S(1)} %get-tuple-element.12), channel_id=1, source_target_pairs={{0,12},{4,8},{8,4},{12,0},{1,13},{5,9},{9,5},{13,1},{2,14},{6,10},... | collective-permute-start | bytes 393224 | tf_op jit(solution)/shard_map/ppermute | solution.py:121
  31.7 2.3 %collective-permute-done.4.refs_0_ = bf16[64,8,128]{2,1,0:T(8,128)(2,1)S(1)} collective-permute-done((bf16[64,8,128]{2,1,0:T(8,128)(2,1)S(1)}, bf16[64,8,128]{2,1,0:T(8,128)(2,1)S(1)}, u32[]{:S(2)}, u32[]{:S(2)}) %collective-permute-start.4) | collective-permute-done | bytes 131104 | tf_op jit(solution)/shard_map/ppermute | solution.py:121
  34.0 4.8 %collective-permute-done.5.refs_1_ = bf16[64,8,128]{2,1,0:T(8,128)(2,1)S(1)} collective-permute-done((bf16[64,8,128]{2,1,0:T(8,128)(2,1)S(1)}, bf16[64,8,128]{2,1,0:T(8,128)(2,1)S(1)}, u32[]{:S(2)}, u32[]{:S(2)}) %collective-permute-start.5) | collective-permute-done | bytes 131104 | tf_op jit(solution)/shard_map/ppermute | solution.py:121
  38.8 0.0 collective-permute-done.6.refs_2_
  38.8 0.0 copy-done.2
  38.8 0.8 %total.1 = f32[64,8,128]{2,1,0:T(8,128)} custom-call(f32[64,8,128]{2,1,0:T(8,128)S(1)} %bitcast.4, f32[64,128]{1,0:T(8,128)S(1)} %bitcast.5, f32[64,8,128]{2,1,0:T(8,128)S(1)} %get-tuple-element.9.own_ref, bf16[64,8,128]{2,1,0:T(8,128)(2,1)S(1)} %collective-permute-done.4.refs_0_, bf16[64,8,128]{2,1,0:T(8,128)(2,1)S(1)} %collective-permute-done.5.refs_1_, ...), custom_call_target="tpu_custom_call" | custom-call | tf_op jit(solution)/shard_map/total/pallas_call | solution.py:122
  (8 shorter events, 0.0 us)
Async XLA Ops:
  0.0 25.9 %copy-start.6 = (f32[8,128]{1,0:T(8,128)S(1)}, f32[8,128]{1,0:T(8,128)}, u32[]{:S(2)}) copy-start(f32[8,128]{1,0:T(8,128)} %weight_ref.1) | copy-start | bytes 12292
  0.0 25.9 %copy-start.5 = (f32[8,128]{1,0:T(8,128)S(1)}, f32[8,128]{1,0:T(8,128)}, u32[]{:S(2)}) copy-start(f32[8,128]{1,0:T(8,128)} %obs_ref.1) | copy-start | bytes 12292
  0.0 38.8 %copy-start.2 = (f32[1,64,8,128]{3,2,1,0:T(8,128)S(1)}, f32[1,64,8,128]{3,2,1,0:T(8,128)}, u32[]{:S(2)}) copy-start(f32[1,64,8,128]{3,2,1,0:T(8,128)} %param.6) | copy-start | bytes 786436
  0.0 38.8 %copy-start.3 = (f32[1,64,128]{2,1,0:T(8,128)S(1)}, f32[1,64,128]{2,1,0:T(8,128)}, u32[]{:S(2)}) copy-start(f32[1,64,128]{2,1,0:T(8,128)} %param.7) | copy-start | bytes 98308
  1.0 9.5 %collective-permute-start.2 = (bf16[64,8,128]{2,1,0:T(8,128)(2,1)S(1)}, bf16[64,8,128]{2,1,0:T(8,128)(2,1)S(1)}, u32[]{:S(2)}, u32[]{:S(2)}) collective-permute-start(bf16[64,8,128]{2,1,0:T(8,128)(2,1)S(1)} %bitcast_convert_fusion.refs_0_), channel_id=1, source_target_pairs={{0,12},{4,8},{8,4},{12,0},{1,13},{5,9},{9,5},{13,1},{2,14},{6,10},... | collective-permute-start | bytes 393224 | tf_op jit(solution)/shard_map/ppermute | solution.py:92
  6.2 11.1 %collective-permute-start.1 = (bf16[64,8,128]{2,1,0:T(8,128)(2,1)S(1)}, bf16[64,8,128]{2,1,0:T(8,128)(2,1)S(1)}, u32[]{:S(2)}, u32[]{:S(2)}) collective-permute-start(bf16[64,8,128]{2,1,0:T(8,128)(2,1)S(1)} %bitcast_convert_fusion.refs_0_), channel_id=1, source_target_pairs={{0,8},{4,12},{8,0},{12,4},{1,9},{5,13},{9,1},{13,5},{2,10},{6,14},... | collective-permute-start | bytes 393224 | tf_op jit(solution)/shard_map/ppermute | solution.py:92
  6.2 11.1 %collective-permute-start = (bf16[64,8,128]{2,1,0:T(8,128)(2,1)S(1)}, bf16[64,8,128]{2,1,0:T(8,128)(2,1)S(1)}, u32[]{:S(2)}, u32[]{:S(2)}) collective-permute-start(bf16[64,8,128]{2,1,0:T(8,128)(2,1)S(1)} %bitcast_convert_fusion.refs_0_), channel_id=1, source_target_pairs={{0,4},{4,0},{8,12},{12,8},{1,5},{5,1},{9,13},{13,9},{2,6},{6,2},{1... | collective-permute-start | bytes 393224 | tf_op jit(solution)/shard_map/ppermute | solution.py:92
  17.2 2.2 %copy-start = (bf16[8,16,128,128]{3,2,1,0:T(8,128)(2,1)S(1)}, bf16[8,16,128,128]{3,2,1,0:T(8,128)(2,1)}, u32[]{:S(2)}) copy-start(bf16[8,16,128,128]{3,2,1,0:T(8,128)(2,1)} %foot_ref.1) | copy-start | bytes 12582916
  19.4 0.7 %copy-start.4 = (s32[8,16]{1,0:T(8,128)S(1)}, s32[8,16]{1,0:T(8,128)}, u32[]{:S(2)}) copy-start(s32[8,16]{1,0:T(8,128)} %ids_ref.3) | copy-start | bytes 1540
  20.1 5.8 %copy-start.1 = (bf16[8,16,128,128]{3,2,1,0:T(8,128)(2,1)S(1)}, bf16[8,16,128,128]{3,2,1,0:T(8,128)(2,1)}, u32[]{:S(2)}) copy-start(bf16[8,16,128,128]{3,2,1,0:T(8,128)(2,1)} %foot_ref.1) | copy-start | bytes 12582916
  21.9 3.9 %collective-permute-start.3 = (f32[8,8,128]{2,1,0:T(8,128)S(1)}, f32[8,8,128]{2,1,0:T(8,128)S(1)}, u32[]{:S(2)}, u32[]{:S(2)}) collective-permute-start(f32[8,8,128]{2,1,0:T(8,128)S(1)} %modeled.1.mine_ref), channel_id=1, source_target_pairs={{0,2},{2,0},{1,3},{3,1},{4,6},{6,4},{5,7},{7,5},{8,10},{10,8},{9,1... | collective-permute-start | bytes 98312 | tf_op jit(solution)/shard_map/ppermute | solution.py:108
  27.2 6.7 %collective-permute-start.4 = (bf16[64,8,128]{2,1,0:T(8,128)(2,1)S(1)}, bf16[64,8,128]{2,1,0:T(8,128)(2,1)S(1)}, u32[]{:S(2)}, u32[]{:S(2)}) collective-permute-start(bf16[64,8,128]{2,1,0:T(8,128)(2,1)S(1)} %get-tuple-element.10), channel_id=1, source_target_pairs={{0,4},{4,0},{8,12},{12,8},{1,5},{5,1},{9,13},{13,9},{2,6},{6,2},{1... | collective-permute-start | bytes 393224 | tf_op jit(solution)/shard_map/ppermute | solution.py:121
  27.3 11.4 %collective-permute-start.5 = (bf16[64,8,128]{2,1,0:T(8,128)(2,1)S(1)}, bf16[64,8,128]{2,1,0:T(8,128)(2,1)S(1)}, u32[]{:S(2)}, u32[]{:S(2)}) collective-permute-start(bf16[64,8,128]{2,1,0:T(8,128)(2,1)S(1)} %get-tuple-element.11), channel_id=1, source_target_pairs={{0,8},{4,12},{8,0},{12,4},{1,9},{5,13},{9,1},{13,5},{2,10},{6,14},... | collective-permute-start | bytes 393224 | tf_op jit(solution)/shard_map/ppermute | solution.py:121
  30.4 8.4 %collective-permute-start.6 = (bf16[64,8,128]{2,1,0:T(8,128)(2,1)S(1)}, bf16[64,8,128]{2,1,0:T(8,128)(2,1)S(1)}, u32[]{:S(2)}, u32[]{:S(2)}) collective-permute-start(bf16[64,8,128]{2,1,0:T(8,128)(2,1)S(1)} %get-tuple-element.12), channel_id=1, source_target_pairs={{0,12},{4,8},{8,4},{12,0},{1,13},{5,9},{9,5},{13,1},{2,14},{6,10},... | collective-permute-start | bytes 393224 | tf_op jit(solution)/shard_map/ppermute | solution.py:121

commit v2 on v1

--- a/solution.py
+++ b/solution.py
@@ -10,26 +10,24 @@
 BF16 = jnp.bfloat16
 F32 = jnp.float32
 VMEM = pl.BlockSpec(memory_space=pltpu.VMEM)
+ANY = pl.BlockSpec(memory_space=pl.ANY)
 SMEM = pl.BlockSpec(memory_space=pltpu.SMEM)
 PARAMS = pltpu.CompilerParams(vmem_limit_bytes=40 << 20)
 
 
-def partner_pairs(n, step):
-    if n & (n - 1) == 0:
-        return [(i, i ^ step) for i in range(n)]
+def shifted_pairs(n, step):
     return [(i, (i + step) % n) for i in range(n)]
 
 
-def slot_of(n, me, owner):
-    if n & (n - 1) == 0:
-        return me ^ owner
-    return lax.rem(me - owner + n, n)
-
-
-def send_slot_of(n, me, owner):
-    if n & (n - 1) == 0:
-        return me ^ owner
-    return lax.rem(owner - me + n, n)
+def stage_kernel(ids_ref, foot_ref, ids_out, foot_out, sems):
+    copies = [
+        pltpu.make_async_copy(foot_ref, foot_out, sems.at[0]),
+        pltpu.make_async_copy(ids_ref, ids_out, sems.at[1]),
+    ]
+    for copy in copies:
+        copy.start()
+    for copy in copies:
+        copy.wait()
 
 
 def modeled_kernel(n, ids_ref, *refs):
@@ -45,7 +43,7 @@
         for k in range(depth):
             t = ids_ref[b, k]
             owner = lax.div(t, tiles)
-            at = slot_of(n, me, owner) * tiles + (t - owner * tiles)
+            at = lax.rem(me - owner + n, n) * tiles + (t - owner * tiles)
             lhs_ref[b, :, pl.ds(k * cells, cells)] = all_ref[at]
         rhs = jnp.concatenate([foot_ref[b, k] for k in range(depth)], axis=1)
         out_ref[b] = lax.dot_general(
@@ -68,7 +66,7 @@
         for k in range(depth):
             t = ids_ref[b, k]
             owner = lax.div(t, tiles)
-            at = send_slot_of(n, me, owner) * tiles + (t - owner * tiles)
+            at = lax.rem(owner - me + n, n) * tiles + (t - owner * tiles)
             dense_ref[at] = terms[:, k * cells : (k + 1) * cells]
     for slot in range(n):
         outs[slot][...] = dense_ref[pl.ds(slot * tiles, tiles)].astype(outs[slot].dtype)
@@ -89,8 +87,23 @@
     tiles, points, cells = flux.shape
     blocks, depth, soundings, _ = footprint.shape
     rounded = flux.astype(BF16)
-    shards = [rounded] + [lax.ppermute(rounded, "snd", partner_pairs(n, s)) for s in range(1, n)]
+    shards = [rounded] + [lax.ppermute(rounded, "snd", shifted_pairs(n, s)) for s in range(1, n)]
 
+    tile_ids, footprint = pl.pallas_call(
+        stage_kernel,
+        out_shape=[
+            jax.ShapeDtypeStruct(tile_ids.shape, tile_ids.dtype),
+            jax.ShapeDtypeStruct(footprint.shape, footprint.dtype),
+        ],
+        in_specs=[ANY] * 2,
+        out_specs=[VMEM] * 2,
+        scratch_shapes=[pltpu.SemaphoreType.DMA((2,))],
+        compiler_params=PARAMS,
+        cost_estimate=pl.CostEstimate(
+            flops=0, transcendentals=0, bytes_accessed=footprint.size * 4
+        ),
+        name="stage",
+    )(tile_ids, footprint)
     mine = pl.pallas_call(
         functools.partial(modeled_kernel, n),
         out_shape=jax.ShapeDtypeStruct((blocks, points, soundings), F32),
@@ -118,7 +131,7 @@
         compiler_params=PARAMS,
         name="terms",
     )(tile_ids, mine, other, observed, obs_weight, footprint)
-    arrived = [lax.ppermute(grads[s], "snd", partner_pairs(n, s)) for s in range(1, n)]
+    arrived = [lax.ppermute(grads[s], "snd", shifted_pairs(n, s)) for s in range(1, n)]
     gradient = pl.pallas_call(
         functools.partial(final_kernel, n),
         out_shape=jax.ShapeDtypeStruct((tiles, points, cells), F32),

time: 39.8 us -> 36.9 us (0.927)
  waiting for transfers between devices: 19.9 us -> 15.1 us
  starting transfers between devices: 11.7 us -> 13.2 us
  Pallas kernels: 3.99 us -> 4.43 us
    ppermute x6, waiting for transfers between devices: 17.5 us -> 12.7 us  [the longest x3 7 us: body(): lax.ppermute(rounded, 'snd', shifted_pairs(n, s))]
    ppermute x6, starting transfers between devices: 10.2 us -> 11.7 us  [the longest x3 6.11 us: body(): lax.ppermute(rounded, 'snd', shifted_pairs(n, s))]
    unnamed x14 -> x12, local copies, waits for them, and re-layouts: 2.89 us -> 2.89 us
  transfers between devices with their start and end apart: 7 -> 7, of which waited for: 5 -> 4; matrix products, arithmetic and copies ran while one was open for 0% -> 0% of each run, Pallas kernels for 0% -> 1%
where the time goes in v2:
time: 36.9 us; the launch traced here: 36.7 us
  waiting for transfers between devices  15.1 us (41%)
  starting transfers between devices  13.2 us (36%)
  Pallas kernels  4.43 us (12%)
  local copies, waits for them, and re-layouts  2.89 us (8%)
  other arithmetic  0.99 us (3%)
    ppermute x3, waiting for transfers between devices, body(): lax.ppermute(rounded, 'snd', shifted_pairs(n, s))  7 us
    ppermute x3, starting transfers between devices, body(): lax.ppermute(rounded, 'snd', shifted_pairs(n, s))  6.11 us
    ppermute x3, waiting for transfers between devices, body(): lax.ppermute(grads[s], 'snd', shifted_pairs(n, s))  5.67 us
    ppermute x3, starting transfers between devices, body(): lax.ppermute(grads[s], 'snd', shifted_pairs(n, s))  5.61 us
    unnamed x12, local copies, waits for them, and re-layouts  2.89 us
    ppermute x1, waiting for transfers between devices, body(): other = lax.ppermute(mine, 'win', [(0, 1), (1, 0)])  2.42 us
    pallas_call x1, Pallas kernels, body(): pl.pallas_call(functools.partial(modeled_kernel, n), out_shape=jax.ShapeD...  1.82 us
    ppermute x1, starting transfers between devices, body(): other = lax.ppermute(mine, 'win', [(0, 1), (1, 0)])  1.51 us
  transfers between devices with their start and end apart: 7, of which 4 were waited for; matrix products, arithmetic and copies ran while one was open for 0% of the time, Pallas kernels for 1%

profile of v2, /device:TPU:0, one launch (start us, length us, event | category | flops | bytes accessed | tf_op | source)
XLA Modules:
  0.0 36.7 jit_solution(9462724807109542636)
XLA Ops:
  0.0 1.0 %bitcast_convert_fusion.refs_0_ = bf16[64,8,128]{2,1,0:T(8,128)(2,1)S(1)} fusion(f32[1,64,8,128]{3,2,1,0:T(8,128)} %param.6), kind=kLoop, calls=%fused_computation | loop fusion | flops 65536 | bytes 393216 | tf_op jit(solution)/shard_map/convert_element_type | solution.py:89
  1.0 5.1 %collective-permute-start.2 = (bf16[64,8,128]{2,1,0:T(8,128)(2,1)S(1)}, bf16[64,8,128]{2,1,0:T(8,128)(2,1)S(1)}, u32[]{:S(2)}, u32[]{:S(2)}) collective-permute-start(bf16[64,8,128]{2,1,0:T(8,128)(2,1)S(1)} %bitcast_convert_fusion.refs_0_), channel_id=1, source_target_pairs={{0,12},{4,0},{8,4},{12,8},{1,13},{5,1},{9,5},{13,9},{2,14},{6,2},{... | collective-permute-start | bytes 393224 | tf_op jit(solution)/shard_map/ppermute | solution.py:90
  6.1 0.0 collective-permute-start.1
  6.1 1.0 %collective-permute-start = (bf16[64,8,128]{2,1,0:T(8,128)(2,1)S(1)}, bf16[64,8,128]{2,1,0:T(8,128)(2,1)S(1)}, u32[]{:S(2)}, u32[]{:S(2)}) collective-permute-start(bf16[64,8,128]{2,1,0:T(8,128)(2,1)S(1)} %bitcast_convert_fusion.refs_0_), channel_id=1, source_target_pairs={{0,4},{4,8},{8,12},{12,0},{1,5},{5,9},{9,13},{13,1},{2,6},{6,10},{... | collective-permute-start | bytes 393224 | tf_op jit(solution)/shard_map/ppermute | solution.py:90
  7.1 2.2 %copy-done = bf16[8,16,128,128]{3,2,1,0:T(8,128)(2,1)S(1)} copy-done((bf16[8,16,128,128]{3,2,1,0:T(8,128)(2,1)S(1)}, bf16[8,16,128,128]{3,2,1,0:T(8,128)(2,1)}, u32[]{:S(2)}) %copy-start) | copy-done | bytes 4194328
  9.3 0.7 %copy-done.3 = s32[8,16]{1,0:T(8,128)S(1)} copy-done((s32[8,16]{1,0:T(8,128)S(1)}, s32[8,16]{1,0:T(8,128)}, u32[]{:S(2)}) %copy-start.3) | copy-done | bytes 536
  10.0 0.3 stage.1
  10.3 0.0 collective-permute-done.2.refs_3_
  10.3 7.0 %collective-permute-done.1.refs_2_ = bf16[64,8,128]{2,1,0:T(8,128)(2,1)S(1)} collective-permute-done((bf16[64,8,128]{2,1,0:T(8,128)(2,1)S(1)}, bf16[64,8,128]{2,1,0:T(8,128)(2,1)S(1)}, u32[]{:S(2)}, u32[]{:S(2)}) %collective-permute-start.1) | collective-permute-done | bytes 131104 | tf_op jit(solution)/shard_map/ppermute | solution.py:90
  17.3 0.0 collective-permute-done.refs_1_
  17.3 1.8 %modeled.1.mine_ref = f32[8,8,128]{2,1,0:T(8,128)S(1)} custom-call(s32[8,16]{1,0:T(8,128)S(1)} %get-tuple-element.11.ids_ref, bf16[64,8,128]{2,1,0:T(8,128)(2,1)S(1)} %bitcast_convert_fusion.refs_0_, bf16[64,8,128]{2,1,0:T(8,128)(2,1)S(1)} %collective-permute-done.refs_1_, bf16[64,8,128]{2,1,0:T(8,128)(2,1)S(1)} %collective-permute-done.1.refs_2_, ...), custom_call_target="tpu_custom_call" | custom-call | tf_op jit(solution)/shard_map/modeled/pallas_call | solution.py:107
  19.1 1.5 %collective-permute-start.3 = (f32[8,8,128]{2,1,0:T(8,128)S(1)}, f32[8,8,128]{2,1,0:T(8,128)S(1)}, u32[]{:S(2)}, u32[]{:S(2)}) collective-permute-start(f32[8,8,128]{2,1,0:T(8,128)S(1)} %modeled.1.mine_ref), channel_id=1, source_target_pairs={{0,2},{2,0},{1,3},{3,1},{4,6},{6,4},{5,7},{7,5},{8,10},{10,8},{9,1... | collective-permute-start | bytes 98312 | tf_op jit(solution)/shard_map/ppermute | solution.py:121
  20.6 2.4 %collective-permute-done.3.other_ref = f32[8,8,128]{2,1,0:T(8,128)S(1)} collective-permute-done((f32[8,8,128]{2,1,0:T(8,128)S(1)}, f32[8,8,128]{2,1,0:T(8,128)S(1)}, u32[]{:S(2)}, u32[]{:S(2)}) %collective-permute-start.3) | collective-permute-done | bytes 32800 | tf_op jit(solution)/shard_map/ppermute | solution.py:121
  23.1 0.0 copy-done.4
  23.1 0.0 copy-done.5
  23.1 1.5 %terms.1 = (f32[64,8,128]{2,1,0:T(8,128)S(1)}, bf16[64,8,128]{2,1,0:T(8,128)(2,1)S(1)}, bf16[64,8,128]{2,1,0:T(8,128)(2,1)S(1)}, bf16[64,8,128]{2,1,0:T(8,128)(2,1)S(1)}) custom-call(s32[8,16]{1,0:T(8,128)S(1)} %get-tuple-element.11.ids_ref, f32[8,8,128]{2,1,0:T(8,128)S(1)} %modeled.1.mine_ref, f32[8,8,128]{2,1,0:T(8,128)S(1)} %collective-permute-done.3.other_ref, ...), custom_call_target="tpu_custom_call" | custom-call | tf_op jit(solution)/shard_map/terms/pallas_call | solution.py:124
  24.6 0.8 %collective-permute-start.4 = (bf16[64,8,128]{2,1,0:T(8,128)(2,1)S(1)}, bf16[64,8,128]{2,1,0:T(8,128)(2,1)S(1)}, u32[]{:S(2)}, u32[]{:S(2)}) collective-permute-start(bf16[64,8,128]{2,1,0:T(8,128)(2,1)S(1)} %get-tuple-element.14), channel_id=1, source_target_pairs={{0,4},{4,8},{8,12},{12,0},{1,5},{5,9},{9,13},{13,1},{2,6},{6,10},{... | collective-permute-start | bytes 393224 | tf_op jit(solution)/shard_map/ppermute | solution.py:134
  25.3 2.0 %collective-permute-start.5 = (bf16[64,8,128]{2,1,0:T(8,128)(2,1)S(1)}, bf16[64,8,128]{2,1,0:T(8,128)(2,1)S(1)}, u32[]{:S(2)}, u32[]{:S(2)}) collective-permute-start(bf16[64,8,128]{2,1,0:T(8,128)(2,1)S(1)} %get-tuple-element.15), channel_id=1, source_target_pairs={{0,8},{4,12},{8,0},{12,4},{1,9},{5,13},{9,1},{13,5},{2,10},{6,14},... | collective-permute-start | bytes 393224 | tf_op jit(solution)/shard_map/ppermute | solution.py:134
  27.3 2.8 %collective-permute-start.6 = (bf16[64,8,128]{2,1,0:T(8,128)(2,1)S(1)}, bf16[64,8,128]{2,1,0:T(8,128)(2,1)S(1)}, u32[]{:S(2)}, u32[]{:S(2)}) collective-permute-start(bf16[64,8,128]{2,1,0:T(8,128)(2,1)S(1)} %get-tuple-element.16), channel_id=1, source_target_pairs={{0,12},{4,0},{8,4},{12,8},{1,13},{5,1},{9,5},{13,9},{2,14},{6,2},{... | collective-permute-start | bytes 393224 | tf_op jit(solution)/shard_map/ppermute | solution.py:134
  30.2 2.7 %collective-permute-done.4.refs_0_ = bf16[64,8,128]{2,1,0:T(8,128)(2,1)S(1)} collective-permute-done((bf16[64,8,128]{2,1,0:T(8,128)(2,1)S(1)}, bf16[64,8,128]{2,1,0:T(8,128)(2,1)S(1)}, u32[]{:S(2)}, u32[]{:S(2)}) %collective-permute-start.4) | collective-permute-done | bytes 131104 | tf_op jit(solution)/shard_map/ppermute | solution.py:134
  32.9 2.9 %collective-permute-done.5.refs_1_ = bf16[64,8,128]{2,1,0:T(8,128)(2,1)S(1)} collective-permute-done((bf16[64,8,128]{2,1,0:T(8,128)(2,1)S(1)}, bf16[64,8,128]{2,1,0:T(8,128)(2,1)S(1)}, u32[]{:S(2)}, u32[]{:S(2)}) %collective-permute-start.5) | collective-permute-done | bytes 131104 | tf_op jit(solution)/shard_map/ppermute | solution.py:134
  35.9 0.0 collective-permute-done.6.refs_2_
  35.9 0.0 copy-done.1
  35.9 0.8 %total.1 = f32[64,8,128]{2,1,0:T(8,128)} custom-call(f32[64,8,128]{2,1,0:T(8,128)S(1)} %bitcast.4, f32[64,128]{1,0:T(8,128)S(1)} %bitcast.5, f32[64,8,128]{2,1,0:T(8,128)S(1)} %get-tuple-element.13.own_ref, bf16[64,8,128]{2,1,0:T(8,128)(2,1)S(1)} %collective-permute-done.4.refs_0_, bf16[64,8,128]{2,1,0:T(8,128)(2,1)S(1)} %collective-permute-done.5.refs_1_, ...), custom_call_target="tpu_custom_call" | custom-call | tf_op jit(solution)/shard_map/total/pallas_call | solution.py:135
  (7 shorter events, 0.0 us)
Async XLA Ops:
  0.0 23.1 %copy-start.4 = (f32[8,128]{1,0:T(8,128)S(1)}, f32[8,128]{1,0:T(8,128)}, u32[]{:S(2)}) copy-start(f32[8,128]{1,0:T(8,128)} %obs_ref.1) | copy-start | bytes 12292
  0.0 23.1 %copy-start.5 = (f32[8,128]{1,0:T(8,128)S(1)}, f32[8,128]{1,0:T(8,128)}, u32[]{:S(2)}) copy-start(f32[8,128]{1,0:T(8,128)} %weight_ref.1) | copy-start | bytes 12292
  1.0 9.3 %collective-permute-start.2 = (bf16[64,8,128]{2,1,0:T(8,128)(2,1)S(1)}, bf16[64,8,128]{2,1,0:T(8,128)(2,1)S(1)}, u32[]{:S(2)}, u32[]{:S(2)}) collective-permute-start(bf16[64,8,128]{2,1,0:T(8,128)(2,1)S(1)} %bitcast_convert_fusion.refs_0_), channel_id=1, source_target_pairs={{0,12},{4,0},{8,4},{12,8},{1,13},{5,1},{9,5},{13,9},{2,14},{6,2},{... | collective-permute-start | bytes 393224 | tf_op jit(solution)/shard_map/ppermute | solution.py:90
  6.1 11.2 %collective-permute-start.1 = (bf16[64,8,128]{2,1,0:T(8,128)(2,1)S(1)}, bf16[64,8,128]{2,1,0:T(8,128)(2,1)S(1)}, u32[]{:S(2)}, u32[]{:S(2)}) collective-permute-start(bf16[64,8,128]{2,1,0:T(8,128)(2,1)S(1)} %bitcast_convert_fusion.refs_0_), channel_id=1, source_target_pairs={{0,8},{4,12},{8,0},{12,4},{1,9},{5,13},{9,1},{13,5},{2,10},{6,14},... | collective-permute-start | bytes 393224 | tf_op jit(solution)/shard_map/ppermute | solution.py:90
  6.1 11.2 %collective-permute-start = (bf16[64,8,128]{2,1,0:T(8,128)(2,1)S(1)}, bf16[64,8,128]{2,1,0:T(8,128)(2,1)S(1)}, u32[]{:S(2)}, u32[]{:S(2)}) collective-permute-start(bf16[64,8,128]{2,1,0:T(8,128)(2,1)S(1)} %bitcast_convert_fusion.refs_0_), channel_id=1, source_target_pairs={{0,4},{4,8},{8,12},{12,0},{1,5},{5,9},{9,13},{13,1},{2,6},{6,10},{... | collective-permute-start | bytes 393224 | tf_op jit(solution)/shard_map/ppermute | solution.py:90
  7.1 2.2 %copy-start = (bf16[8,16,128,128]{3,2,1,0:T(8,128)(2,1)S(1)}, bf16[8,16,128,128]{3,2,1,0:T(8,128)(2,1)}, u32[]{:S(2)}) copy-start(bf16[8,16,128,128]{3,2,1,0:T(8,128)(2,1)} %foot_ref.1) | copy-start | bytes 12582916
  9.3 0.7 %copy-start.3 = (s32[8,16]{1,0:T(8,128)S(1)}, s32[8,16]{1,0:T(8,128)}, u32[]{:S(2)}) copy-start(s32[8,16]{1,0:T(8,128)} %ids_ref.1) | copy-start | bytes 1540
  17.3 18.6 %copy-start.1 = (f32[1,64,8,128]{3,2,1,0:T(8,128)S(1)}, f32[1,64,8,128]{3,2,1,0:T(8,128)}, u32[]{:S(2)}) copy-start(f32[1,64,8,128]{3,2,1,0:T(8,128)} %param.6) | copy-start | bytes 786436
  17.3 18.6 %copy-start.2 = (f32[1,64,128]{2,1,0:T(8,128)S(1)}, f32[1,64,128]{2,1,0:T(8,128)}, u32[]{:S(2)}) copy-start(f32[1,64,128]{2,1,0:T(8,128)} %param.7) | copy-start | bytes 98308
  19.1 3.9 %collective-permute-start.3 = (f32[8,8,128]{2,1,0:T(8,128)S(1)}, f32[8,8,128]{2,1,0:T(8,128)S(1)}, u32[]{:S(2)}, u32[]{:S(2)}) collective-permute-start(f32[8,8,128]{2,1,0:T(8,128)S(1)} %modeled.1.mine_ref), channel_id=1, source_target_pairs={{0,2},{2,0},{1,3},{3,1},{4,6},{6,4},{5,7},{7,5},{8,10},{10,8},{9,1... | collective-permute-start | bytes 98312 | tf_op jit(solution)/shard_map/ppermute | solution.py:121
  24.6 8.3 %collective-permute-start.4 = (bf16[64,8,128]{2,1,0:T(8,128)(2,1)S(1)}, bf16[64,8,128]{2,1,0:T(8,128)(2,1)S(1)}, u32[]{:S(2)}, u32[]{:S(2)}) collective-permute-start(bf16[64,8,128]{2,1,0:T(8,128)(2,1)S(1)} %get-tuple-element.14), channel_id=1, source_target_pairs={{0,4},{4,8},{8,12},{12,0},{1,5},{5,9},{9,13},{13,1},{2,6},{6,10},{... | collective-permute-start | bytes 393224 | tf_op jit(solution)/shard_map/ppermute | solution.py:134
  25.3 10.5 %collective-permute-start.5 = (bf16[64,8,128]{2,1,0:T(8,128)(2,1)S(1)}, bf16[64,8,128]{2,1,0:T(8,128)(2,1)S(1)}, u32[]{:S(2)}, u32[]{:S(2)}) collective-permute-start(bf16[64,8,128]{2,1,0:T(8,128)(2,1)S(1)} %get-tuple-element.15), channel_id=1, source_target_pairs={{0,8},{4,12},{8,0},{12,4},{1,9},{5,13},{9,1},{13,5},{2,10},{6,14},... | collective-permute-start | bytes 393224 | tf_op jit(solution)/shard_map/ppermute | solution.py:134
  27.3 8.5 %collective-permute-start.6 = (bf16[64,8,128]{2,1,0:T(8,128)(2,1)S(1)}, bf16[64,8,128]{2,1,0:T(8,128)(2,1)S(1)}, u32[]{:S(2)}, u32[]{:S(2)}) collective-permute-start(bf16[64,8,128]{2,1,0:T(8,128)(2,1)S(1)} %get-tuple-element.16), channel_id=1, source_target_pairs={{0,12},{4,0},{8,4},{12,8},{1,13},{5,1},{9,5},{13,9},{2,14},{6,2},{... | collective-permute-start | bytes 393224 | tf_op jit(solution)/shard_map/ppermute | solution.py:134

commit v3 on v2

v3 whole, which is shorter than its diff:
```python
import functools

import jax
import jax.numpy as jnp
from jax import lax
from jax.experimental import pallas as pl
from jax.experimental.pallas import tpu as pltpu
from jax.sharding import PartitionSpec as P

BF16 = jnp.bfloat16
F32 = jnp.float32
I32 = jnp.int32
HBM = pl.BlockSpec(memory_space=pltpu.HBM)
VMEM = pl.BlockSpec(memory_space=pltpu.VMEM)
PARAMS = pltpu.CompilerParams(vmem_limit_bytes=40 << 20)
PIECES = 4


def shifted_pairs(n, step):
    return [(i, (i + step) % n) for i in range(n)]


def struct(shape, dtype):
    return jax.ShapeDtypeStruct(shape, dtype)


def in_hbm(x):
    return pltpu.with_memory_space_constraint(x, pltpu.HBM)


def round_kernel(flux_ref, out_ref, buf_ref, sems):
    size = flux_ref.shape[0] // PIECES
    pieces = [pl.ds(i * size, size) for i in range(PIECES)]
    copies = [
        pltpu.make_async_copy(flux_ref.at[at], buf_ref.at[at], sems.at[i]) for i, at in enumerate(pieces)
    ]
    for copy in copies:
        copy.start()
    for copy, at in zip(copies, pieces):
        copy.wait()
        out_ref[at] = buf_ref[at].astype(BF16)


def stage_kernel(n, tiles, ids_ref, foot_ref, take_ref, put_ref, foot_out, turned_ref, sems):
    blocks, depth = ids_ref.shape
    copies = [pltpu.make_async_copy(foot_ref.at[b], foot_out.at[b], sems.at[b]) for b in range(blocks)]
    for copy in copies:
        copy.start()
    me = lax.axis_index("snd")
    ids = ids_ref[...]
    shift = tiles.bit_length() - 1
    owner = lax.shift_right_logical(ids, shift)
    local = ids - lax.shift_left(owner, shift)
    slot = me - owner
    take_ref[...] = jnp.where(slot < 0, slot + n, slot) * tiles + local
    slot = owner - me
    put_ref[...] = jnp.where(slot < 0, slot + n, slot) * tiles + local
    for b in range(blocks):
        copies[b].wait()
        turned_ref[b] = jnp.swapaxes(foot_out[b], 1, 2)


def modeled_kernel(n, take_ref, turned_ref, *refs):
    shards = refs[:n]
    out_ref, all_ref = refs[n:]
    tiles = shards[0].shape[0]
    blocks, depth = take_ref.shape
    for slot in range(n):
        all_ref[pl.ds(slot * tiles, tiles)] = shards[slot][...]
    take = take_ref[...]
    for b in range(blocks):
        lhs = jnp.concatenate([all_ref[take[b, k]] for k in range(depth)], axis=1)
        rhs = jnp.concatenate([turned_ref[b, k] for k in range(depth)], axis=0)
        out_ref[b] = jnp.dot(lhs, rhs, preferred_element_type=F32)


def terms_kernel(n, put_ref, mine_ref, other_ref, obs_ref, weight_ref, foot_ref, *refs):
    outs, dense_ref = refs[:n], refs[n]
    tiles = outs[0].shape[0]
    blocks, depth, _, cells = foot_ref.shape
    dense_ref[...] = jnp.zeros_like(dense_ref)
    put = put_ref[...]
    for b in range(blocks):
        modeled = mine_ref[b] + other_ref[b]
        resid = (weight_ref[pl.ds(b, 1), :] * (modeled - obs_ref[pl.ds(b, 1), :])).astype(BF16)
        rhs = jnp.concatenate([foot_ref[b, k] for k in range(depth)], axis=1)
        terms = jnp.dot(resid, rhs, preferred_element_type=F32)
        for k in range(depth):
            dense_ref[put[b, k]] = terms[:, k * cells : (k + 1) * cells]
    for slot in range(n):
        outs[slot][...] = dense_ref[pl.ds(slot * tiles, tiles)].astype(outs[slot].dtype)


def total_kernel(n, flux_ref, prior_ref, own_ref, *refs):
    arrived, out_ref = refs[: n - 1], refs[n - 1]
    total = own_ref[...] + prior_ref[...][:, None, :] * flux_ref[...]
    for a in arrived:
        total += a[...].astype(F32)
    out_ref[...] = total


def body(flux_state, prior_precision, footprint, tile_ids, observed, obs_weight):
    n = lax.axis_size("snd")
    windows = lax.axis_size("win")
    flux = flux_state[0]
    tiles, points, cells = flux.shape
    blocks, depth, soundings, _ = footprint.shape
    assert tiles & (tiles - 1) == 0 and tiles % PIECES == 0
    held = (tiles, points, cells)

    rounded = pl.pallas_call(
        round_kernel,
        out_shape=struct(held, BF16),
        in_specs=[HBM],
        out_specs=VMEM,
        scratch_shapes=[pltpu.VMEM(held, F32), pltpu.SemaphoreType.DMA((PIECES,))],
        compiler_params=PARAMS,
        name="round",
    )(in_hbm(flux))
    shards = [rounded] + [lax.ppermute(rounded, "snd", shifted_pairs(n, s)) for s in range(1, n)]
    take, put, foot, turned = pl.pallas_call(
        functools.partial(stage_kernel, n, tiles),
        out_shape=[struct(tile_ids.shape, I32)] * 2 + [struct(footprint.shape, BF16)] * 2,
        in_specs=[VMEM, HBM],
        out_specs=[VMEM] * 4,
        scratch_shapes=[pltpu.SemaphoreType.DMA((blocks,))],
        compiler_params=PARAMS,
        cost_estimate=pl.CostEstimate(flops=0, transcendentals=0, bytes_accessed=footprint.size * 4),
        name="stage",
    )(tile_ids, in_hbm(footprint))
    mine = pl.pallas_call(
        functools.partial(modeled_kernel, n),
        out_shape=struct((blocks, points, soundings), F32),
        in_specs=[VMEM] * (n + 2),
        out_specs=VMEM,
        scratch_shapes=[pltpu.VMEM((n * tiles, points, cells), BF16)],
        compiler_params=PARAMS,
        name="modeled",
    )(take, turned, *shards)
    if windows == 2:
        other = lax.ppermute(mine, "win", [(0, 1), (1, 0)])
    else:
        other = lax.psum(mine, "win") - mine
    terms = pl.pallas_call(
        functools.partial(terms_kernel, n),
        out_shape=[struct(held, F32)] + [struct(held, BF16)] * (n - 1),
        in_specs=[VMEM] * 6,
        out_specs=[VMEM] * n,
        scratch_shapes=[pltpu.VMEM((n * tiles, points, cells), F32)],
        compiler_params=PARAMS,
        name="terms",
    )(put, mine, other, observed, obs_weight, foot)
    arrived = [lax.ppermute(terms[s], "snd", shifted_pairs(n, s)) for s in range(1, n)]
    gradient = pl.pallas_call(
        functools.partial(total_kernel, n),
        out_shape=struct(held, F32),
        in_specs=[VMEM] * (n + 2),
        out_specs=VMEM,
        compiler_params=PARAMS,
        name="total",
    )(flux, prior_precision[0], terms[0], *arrived)
    return gradient[None]


def solution(mesh):
    placed = (
        P(("groups", "win"), "snd", "pt", None),
        P(("groups", "win"), "snd", None),
        P(("groups", "snd"), "win", None, None),
        P(("groups", "snd"), "win"),
        P(("groups", "snd"), None),
        P(("groups", "snd"), None),
    )
    return jax.shard_map(
        body,
        mesh=mesh,
        in_specs=placed,
        out_specs=P(("groups", "win"), "snd", "pt", None),
        check_vma=False,
    )
```

time: 36.9 us -> 35.1 us (0.951)
  local copies, waits for them, and re-layouts: 2.89 us -> 0.7 us
  Pallas kernels: 4.43 us -> 5.92 us
  other arithmetic: 0.99 us -> 0 us
    unnamed x12 -> x10, local copies, waits for them, and re-layouts: 2.89 us -> 0.7 us
    pallas_call x4 -> x5, Pallas kernels: 4.43 us -> 5.92 us  [the longest x1 2.64 us: body(): pl.pallas_call(functools.partial(stage_kernel, n, tiles), out_shape=[stru...]
    convert_element_type x1 -> x0, other arithmetic: 0.99 us -> none  [body(): rounded = flux.astype(BF16)]
  transfers between devices with their start and end apart: 7 -> 7, of which waited for: 4 -> 4; matrix products, arithmetic and copies ran while one was open for 0% -> 0% of each run, Pallas kernels for 1% -> 8%
where the time goes in v3:
time: 35.1 us; the launch traced here: 34.9 us
  waiting for transfers between devices  15 us (43%)
  starting transfers between devices  13.3 us (38%)
  Pallas kernels  5.92 us (17%)
  local copies, waits for them, and re-layouts  0.7 us (2%)
    ppermute x3, waiting for transfers between devices, body(): lax.ppermute(rounded, 'snd', shifted_pairs(n, s))  6.85 us
    ppermute x3, starting transfers between devices, body(): lax.ppermute(rounded, 'snd', shifted_pairs(n, s))  6.11 us
    ppermute x3, waiting for transfers between devices, body(): lax.ppermute(terms[s], 'snd', shifted_pairs(n, s))  5.67 us
    ppermute x3, starting transfers between devices, body(): lax.ppermute(terms[s], 'snd', shifted_pairs(n, s))  5.6 us
    pallas_call x1, Pallas kernels, body(): pl.pallas_call(functools.partial(stage_kernel, n, tiles), out_shape=[stru...  2.64 us
    ppermute x1, waiting for transfers between devices, body(): other = lax.ppermute(mine, 'win', [(0, 1), (1, 0)])  2.42 us
    ppermute x1, starting transfers between devices, body(): other = lax.ppermute(mine, 'win', [(0, 1), (1, 0)])  1.55 us
    pallas_call x1, Pallas kernels, body(): pl.pallas_call(round_kernel, out_shape=struct(held, BF16), in_specs=[HBM]...  1 us
  transfers between devices with their start and end apart: 7, of which 4 were waited for; matrix products, arithmetic and copies ran while one was open for 0% of the time, Pallas kernels for 8%

profile of v3, /device:TPU:0, one launch (start us, length us, event | category | flops | bytes accessed | tf_op | source)
XLA Modules:
  0.0 34.9 jit_solution(17181737430585139562)
XLA Ops:
  0.0 1.0 %round.1.refs_0_ = bf16[64,8,128]{2,1,0:T(8,128)(2,1)S(1)} custom-call(f32[64,8,128]{2,1,0:T(8,128)} %bitcast.3), custom_call_target="tpu_custom_call" | custom-call | tf_op jit(solution)/shard_map/round/pallas_call | solution.py:111
  1.0 5.1 %collective-permute-start.2 = (bf16[64,8,128]{2,1,0:T(8,128)(2,1)S(1)}, bf16[64,8,128]{2,1,0:T(8,128)(2,1)S(1)}, u32[]{:S(2)}, u32[]{:S(2)}) collective-permute-start(bf16[64,8,128]{2,1,0:T(8,128)(2,1)S(1)} %round.1.refs_0_), channel_id=1, source_target_pairs={{0,12},{4,0},{8,4},{12,8},{1,13},{5,1},{9,5},{13,9},{2,14},{6,2},{... | collective-permute-start | bytes 393224 | tf_op jit(solution)/shard_map/ppermute | solution.py:120
  6.1 0.0 collective-permute-start.1
  6.1 1.0 %collective-permute-start = (bf16[64,8,128]{2,1,0:T(8,128)(2,1)S(1)}, bf16[64,8,128]{2,1,0:T(8,128)(2,1)S(1)}, u32[]{:S(2)}, u32[]{:S(2)}) collective-permute-start(bf16[64,8,128]{2,1,0:T(8,128)(2,1)S(1)} %round.1.refs_0_), channel_id=1, source_target_pairs={{0,4},{4,8},{8,12},{12,0},{1,5},{5,9},{9,13},{13,1},{2,6},{6,10},{... | collective-permute-start | bytes 393224 | tf_op jit(solution)/shard_map/ppermute | solution.py:120
  7.1 0.7 %copy-done.2 = s32[8,16]{1,0:T(8,128)S(1)} copy-done((s32[8,16]{1,0:T(8,128)S(1)}, s32[8,16]{1,0:T(8,128)}, u32[]{:S(2)}) %copy-start.2) | copy-done | bytes 536
  7.8 2.6 %stage.1 = (s32[8,16]{1,0:T(8,128)S(1)}, s32[8,16]{1,0:T(8,128)S(1)}, bf16[8,16,128,128]{3,2,1,0:T(8,128)(2,1)S(1)}, bf16[8,16,128,128]{3,2,1,0:T(8,128)(2,1)S(1)}) custom-call(s32[8,16]{1,0:T(8,128)S(1)} %copy-done.2, bf16[8,16,128,128]{3,2,1,0:T(8,128)(2,1)} %foot_ref.1), custom_call_target="tpu_custom_call" | custom-call | bytes 8388608 | tf_op jit(solution)/shard_map/stage/pallas_call | solution.py:121
  10.5 0.0 collective-permute-done.2.refs_3_
  10.5 6.8 %collective-permute-done.1.refs_2_ = bf16[64,8,128]{2,1,0:T(8,128)(2,1)S(1)} collective-permute-done((bf16[64,8,128]{2,1,0:T(8,128)(2,1)S(1)}, bf16[64,8,128]{2,1,0:T(8,128)(2,1)S(1)}, u32[]{:S(2)}, u32[]{:S(2)}) %collective-permute-start.1) | collective-permute-done | bytes 131104 | tf_op jit(solution)/shard_map/ppermute | solution.py:120
  17.3 0.0 collective-permute-done.refs_1_
  17.3 0.7 %modeled.1.mine_ref = f32[8,8,128]{2,1,0:T(8,128)S(1)} custom-call(s32[8,16]{1,0:T(8,128)S(1)} %get-tuple-element.14.take_ref, bf16[8,16,128,128]{3,2,1,0:T(8,128)(2,1)S(1)} %get-tuple-element.15.turned_ref, bf16[64,8,128]{2,1,0:T(8,128)(2,1)S(1)} %round.1.refs_0_, bf16[64,8,128]{2,1,0:T(8,128)(2,1)S(1)} %collective-permute-done.refs_1_, ...), custom_call_target="tpu_custom_call" | custom-call | tf_op jit(solution)/shard_map/modeled/pallas_call | solution.py:131
  18.1 1.6 %collective-permute-start.3 = (f32[8,8,128]{2,1,0:T(8,128)S(1)}, f32[8,8,128]{2,1,0:T(8,128)S(1)}, u32[]{:S(2)}, u32[]{:S(2)}) collective-permute-start(f32[8,8,128]{2,1,0:T(8,128)S(1)} %modeled.1.mine_ref), channel_id=1, source_target_pairs={{0,2},{2,0},{1,3},{3,1},{4,6},{6,4},{5,7},{7,5},{8,10},{10,8},{9,1... | collective-permute-start | bytes 98312 | tf_op jit(solution)/shard_map/ppermute | solution.py:141
  19.6 2.4 %collective-permute-done.3.other_ref = f32[8,8,128]{2,1,0:T(8,128)S(1)} collective-permute-done((f32[8,8,128]{2,1,0:T(8,128)S(1)}, f32[8,8,128]{2,1,0:T(8,128)S(1)}, u32[]{:S(2)}, u32[]{:S(2)}) %collective-permute-start.3) | collective-permute-done | bytes 32800 | tf_op jit(solution)/shard_map/ppermute | solution.py:141
  22.1 0.0 copy-done.3
  22.1 0.0 copy-done.4
  22.1 0.7 %terms.1 = (f32[64,8,128]{2,1,0:T(8,128)S(1)}, bf16[64,8,128]{2,1,0:T(8,128)(2,1)S(1)}, bf16[64,8,128]{2,1,0:T(8,128)(2,1)S(1)}, bf16[64,8,128]{2,1,0:T(8,128)(2,1)S(1)}) custom-call(s32[8,16]{1,0:T(8,128)S(1)} %get-tuple-element.13.put_ref, f32[8,8,128]{2,1,0:T(8,128)S(1)} %modeled.1.mine_ref, f32[8,8,128]{2,1,0:T(8,128)S(1)} %collective-permute-done.3.other_ref, ...), custom_call_target="tpu_custom_call" | custom-call | tf_op jit(solution)/shard_map/terms/pallas_call | solution.py:144
  22.8 0.8 %collective-permute-start.4 = (bf16[64,8,128]{2,1,0:T(8,128)(2,1)S(1)}, bf16[64,8,128]{2,1,0:T(8,128)(2,1)S(1)}, u32[]{:S(2)}, u32[]{:S(2)}) collective-permute-start(bf16[64,8,128]{2,1,0:T(8,128)(2,1)S(1)} %get-tuple-element.18), channel_id=1, source_target_pairs={{0,4},{4,8},{8,12},{12,0},{1,5},{5,9},{9,13},{13,1},{2,6},{6,10},{... | collective-permute-start | bytes 393224 | tf_op jit(solution)/shard_map/ppermute | solution.py:153
  23.6 2.0 %collective-permute-start.5 = (bf16[64,8,128]{2,1,0:T(8,128)(2,1)S(1)}, bf16[64,8,128]{2,1,0:T(8,128)(2,1)S(1)}, u32[]{:S(2)}, u32[]{:S(2)}) collective-permute-start(bf16[64,8,128]{2,1,0:T(8,128)(2,1)S(1)} %get-tuple-element.19), channel_id=1, source_target_pairs={{0,8},{4,12},{8,0},{12,4},{1,9},{5,13},{9,1},{13,5},{2,10},{6,14},... | collective-permute-start | bytes 393224 | tf_op jit(solution)/shard_map/ppermute | solution.py:153
  25.6 2.8 %collective-permute-start.6 = (bf16[64,8,128]{2,1,0:T(8,128)(2,1)S(1)}, bf16[64,8,128]{2,1,0:T(8,128)(2,1)S(1)}, u32[]{:S(2)}, u32[]{:S(2)}) collective-permute-start(bf16[64,8,128]{2,1,0:T(8,128)(2,1)S(1)} %get-tuple-element.20), channel_id=1, source_target_pairs={{0,12},{4,0},{8,4},{12,8},{1,13},{5,1},{9,5},{13,9},{2,14},{6,2},{... | collective-permute-start | bytes 393224 | tf_op jit(solution)/shard_map/ppermute | solution.py:153
  28.4 2.7 %collective-permute-done.4.refs_0_ = bf16[64,8,128]{2,1,0:T(8,128)(2,1)S(1)} collective-permute-done((bf16[64,8,128]{2,1,0:T(8,128)(2,1)S(1)}, bf16[64,8,128]{2,1,0:T(8,128)(2,1)S(1)}, u32[]{:S(2)}, u32[]{:S(2)}) %collective-permute-start.4) | collective-permute-done | bytes 131104 | tf_op jit(solution)/shard_map/ppermute | solution.py:153
  31.2 2.9 %collective-permute-done.5.refs_1_ = bf16[64,8,128]{2,1,0:T(8,128)(2,1)S(1)} collective-permute-done((bf16[64,8,128]{2,1,0:T(8,128)(2,1)S(1)}, bf16[64,8,128]{2,1,0:T(8,128)(2,1)S(1)}, u32[]{:S(2)}, u32[]{:S(2)}) %collective-permute-start.5) | collective-permute-done | bytes 131104 | tf_op jit(solution)/shard_map/ppermute | solution.py:153
  34.1 0.0 collective-permute-done.6.refs_2_
  34.1 0.0 copy-done
  34.1 0.0 copy-done.1
  34.1 0.8 %total.1 = f32[64,8,128]{2,1,0:T(8,128)} custom-call(f32[64,8,128]{2,1,0:T(8,128)S(1)} %bitcast.4, f32[64,128]{1,0:T(8,128)S(1)} %bitcast.5, f32[64,8,128]{2,1,0:T(8,128)S(1)} %get-tuple-element.17.own_ref, bf16[64,8,128]{2,1,0:T(8,128)(2,1)S(1)} %collective-permute-done.4.refs_0_, bf16[64,8,128]{2,1,0:T(8,128)(2,1)S(1)} %collective-permute-done.5.refs_1_, ...), custom_call_target="tpu_custom_call" | custom-call | tf_op jit(solution)/shard_map/total/pallas_call | solution.py:154
  (5 shorter events, 0.0 us)
Async XLA Ops:
  0.0 22.1 %copy-start.3 = (f32[8,128]{1,0:T(8,128)S(1)}, f32[8,128]{1,0:T(8,128)}, u32[]{:S(2)}) copy-start(f32[8,128]{1,0:T(8,128)} %obs_ref.1) | copy-start | bytes 12292
  0.0 22.1 %copy-start.4 = (f32[8,128]{1,0:T(8,128)S(1)}, f32[8,128]{1,0:T(8,128)}, u32[]{:S(2)}) copy-start(f32[8,128]{1,0:T(8,128)} %weight_ref.1) | copy-start | bytes 12292
  1.0 9.4 %collective-permute-start.2 = (bf16[64,8,128]{2,1,0:T(8,128)(2,1)S(1)}, bf16[64,8,128]{2,1,0:T(8,128)(2,1)S(1)}, u32[]{:S(2)}, u32[]{:S(2)}) collective-permute-start(bf16[64,8,128]{2,1,0:T(8,128)(2,1)S(1)} %round.1.refs_0_), channel_id=1, source_target_pairs={{0,12},{4,0},{8,4},{12,8},{1,13},{5,1},{9,5},{13,9},{2,14},{6,2},{... | collective-permute-start | bytes 393224 | tf_op jit(solution)/shard_map/ppermute | solution.py:120
  6.1 11.2 %collective-permute-start.1 = (bf16[64,8,128]{2,1,0:T(8,128)(2,1)S(1)}, bf16[64,8,128]{2,1,0:T(8,128)(2,1)S(1)}, u32[]{:S(2)}, u32[]{:S(2)}) collective-permute-start(bf16[64,8,128]{2,1,0:T(8,128)(2,1)S(1)} %round.1.refs_0_), channel_id=1, source_target_pairs={{0,8},{4,12},{8,0},{12,4},{1,9},{5,13},{9,1},{13,5},{2,10},{6,14},... | collective-permute-start | bytes 393224 | tf_op jit(solution)/shard_map/ppermute | solution.py:120
  6.1 11.2 %collective-permute-start = (bf16[64,8,128]{2,1,0:T(8,128)(2,1)S(1)}, bf16[64,8,128]{2,1,0:T(8,128)(2,1)S(1)}, u32[]{:S(2)}, u32[]{:S(2)}) collective-permute-start(bf16[64,8,128]{2,1,0:T(8,128)(2,1)S(1)} %round.1.refs_0_), channel_id=1, source_target_pairs={{0,4},{4,8},{8,12},{12,0},{1,5},{5,9},{9,13},{13,1},{2,6},{6,10},{... | collective-permute-start | bytes 393224 | tf_op jit(solution)/shard_map/ppermute | solution.py:120
  7.1 0.7 %copy-start.2 = (s32[8,16]{1,0:T(8,128)S(1)}, s32[8,16]{1,0:T(8,128)}, u32[]{:S(2)}) copy-start(s32[8,16]{1,0:T(8,128)} %ids_ref.1) | copy-start | bytes 1540
  17.3 16.8 %copy-start = (f32[1,64,8,128]{3,2,1,0:T(8,128)S(1)}, f32[1,64,8,128]{3,2,1,0:T(8,128)}, u32[]{:S(2)}) copy-start(f32[1,64,8,128]{3,2,1,0:T(8,128)} %param.6) | copy-start | bytes 786436
  17.3 16.8 %copy-start.1 = (f32[1,64,128]{2,1,0:T(8,128)S(1)}, f32[1,64,128]{2,1,0:T(8,128)}, u32[]{:S(2)}) copy-start(f32[1,64,128]{2,1,0:T(8,128)} %param.7) | copy-start | bytes 98308
  18.1 4.0 %collective-permute-start.3 = (f32[8,8,128]{2,1,0:T(8,128)S(1)}, f32[8,8,128]{2,1,0:T(8,128)S(1)}, u32[]{:S(2)}, u32[]{:S(2)}) collective-permute-start(f32[8,8,128]{2,1,0:T(8,128)S(1)} %modeled.1.mine_ref), channel_id=1, source_target_pairs={{0,2},{2,0},{1,3},{3,1},{4,6},{6,4},{5,7},{7,5},{8,10},{10,8},{9,1... | collective-permute-start | bytes 98312 | tf_op jit(solution)/shard_map/ppermute | solution.py:141
  22.8 8.3 %collective-permute-start.4 = (bf16[64,8,128]{2,1,0:T(8,128)(2,1)S(1)}, bf16[64,8,128]{2,1,0:T(8,128)(2,1)S(1)}, u32[]{:S(2)}, u32[]{:S(2)}) collective-permute-start(bf16[64,8,128]{2,1,0:T(8,128)(2,1)S(1)} %get-tuple-element.18), channel_id=1, source_target_pairs={{0,4},{4,8},{8,12},{12,0},{1,5},{5,9},{9,13},{13,1},{2,6},{6,10},{... | collective-permute-start | bytes 393224 | tf_op jit(solution)/shard_map/ppermute | solution.py:153
  23.6 10.5 %collective-permute-start.5 = (bf16[64,8,128]{2,1,0:T(8,128)(2,1)S(1)}, bf16[64,8,128]{2,1,0:T(8,128)(2,1)S(1)}, u32[]{:S(2)}, u32[]{:S(2)}) collective-permute-start(bf16[64,8,128]{2,1,0:T(8,128)(2,1)S(1)} %get-tuple-element.19), channel_id=1, source_target_pairs={{0,8},{4,12},{8,0},{12,4},{1,9},{5,13},{9,1},{13,5},{2,10},{6,14},... | collective-permute-start | bytes 393224 | tf_op jit(solution)/shard_map/ppermute | solution.py:153
  25.6 8.5 %collective-permute-start.6 = (bf16[64,8,128]{2,1,0:T(8,128)(2,1)S(1)}, bf16[64,8,128]{2,1,0:T(8,128)(2,1)S(1)}, u32[]{:S(2)}, u32[]{:S(2)}) collective-permute-start(bf16[64,8,128]{2,1,0:T(8,128)(2,1)S(1)} %get-tuple-element.20), channel_id=1, source_target_pairs={{0,12},{4,0},{8,4},{12,8},{1,13},{5,1},{9,5},{13,9},{2,14},{6,2},{... | collective-permute-start | bytes 393224 | tf_op jit(solution)/shard_map/ppermute | solution.py:153

commit v4 on v3

--- a/solution.py
+++ b/solution.py
@@ -16,8 +16,40 @@
 PIECES = 4
 
 
-def shifted_pairs(n, step):
-    return [(i, (i + step) % n) for i in range(n)]
+NEXT, ACROSS, LAST = (1, 2, 3, 0), (2, 3, 0, 1), (3, 0, 1, 2)
+CYCLE, MIRROR, BACK = (2, 0, 3, 1), (3, 2, 1, 0), (1, 3, 0, 2)
+
+
+def plans(n, cores):
+    if n == 4 and cores == 2:
+        shifts = (NEXT, ACROSS, LAST)
+        return (shifts, (CYCLE, MIRROR, BACK)), (shifts, (MIRROR, BACK, CYCLE))
+    shifts = tuple(tuple((i + s) % n for i in range(n)) for s in range(1, n))
+    return (shifts,) * cores, (shifts,) * cores
+
+
+def sent(x, plan, step):
+    cores = len(plan)
+    pairs = [(i * cores + c, to * cores + c) for c, steps in enumerate(plan) for i, to in enumerate(steps[step])]
+    return lax.ppermute(x, ("snd", "pt"), pairs)
+
+
+def slots(plan, owner, arriving):
+    n = len(plan[0]) + 1
+    me, core = lax.axis_index("snd"), lax.axis_index("pt")
+    if all(to == tuple((i + s + 1) % n for i in range(n)) for steps in plan for s, to in enumerate(steps)):
+        slot = me - owner if arriving else owner - me
+        return jnp.where(slot < 0, slot + n, slot)
+    slot = jnp.zeros_like(owner)
+    for other in range(n):
+        step = jnp.int32(0)
+        for c, steps in enumerate(plan):
+            for s, to in enumerate(steps):
+                source = to.index(other)
+                here = to[other] if arriving else source
+                step = jnp.where((core == c) & (me == here), s + 1, step)
+        slot = jnp.where(owner == other, step, slot)
+    return slot
 
 
 def struct(shape, dtype):
@@ -41,20 +73,17 @@
         out_ref[at] = buf_ref[at].astype(BF16)
 
 
-def stage_kernel(n, tiles, ids_ref, foot_ref, take_ref, put_ref, foot_out, turned_ref, sems):
+def stage_kernel(gather, spread, tiles, ids_ref, foot_ref, take_ref, put_ref, foot_out, turned_ref, sems):
     blocks, depth = ids_ref.shape
     copies = [pltpu.make_async_copy(foot_ref.at[b], foot_out.at[b], sems.at[b]) for b in range(blocks)]
     for copy in copies:
         copy.start()
-    me = lax.axis_index("snd")
     ids = ids_ref[...]
     shift = tiles.bit_length() - 1
     owner = lax.shift_right_logical(ids, shift)
     local = ids - lax.shift_left(owner, shift)
-    slot = me - owner
-    take_ref[...] = jnp.where(slot < 0, slot + n, slot) * tiles + local
-    slot = owner - me
-    put_ref[...] = jnp.where(slot < 0, slot + n, slot) * tiles + local
+    take_ref[...] = slots(gather, owner, True) * tiles + local
+    put_ref[...] = slots(spread, owner, False) * tiles + local
     for b in range(blocks):
         copies[b].wait()
         turned_ref[b] = jnp.swapaxes(foot_out[b], 1, 2)
@@ -117,9 +146,10 @@
         compiler_params=PARAMS,
         name="round",
     )(in_hbm(flux))
-    shards = [rounded] + [lax.ppermute(rounded, "snd", shifted_pairs(n, s)) for s in range(1, n)]
+    gather, spread = plans(n, lax.axis_size("pt"))
+    shards = [rounded] + [sent(rounded, gather, s) for s in range(n - 1)]
     take, put, foot, turned = pl.pallas_call(
-        functools.partial(stage_kernel, n, tiles),
+        functools.partial(stage_kernel, gather, spread, tiles),
         out_shape=[struct(tile_ids.shape, I32)] * 2 + [struct(footprint.shape, BF16)] * 2,
         in_specs=[VMEM, HBM],
         out_specs=[VMEM] * 4,
@@ -150,7 +180,7 @@
         compiler_params=PARAMS,
         name="terms",
     )(put, mine, other, observed, obs_weight, foot)
-    arrived = [lax.ppermute(terms[s], "snd", shifted_pairs(n, s)) for s in range(1, n)]
+    arrived = [sent(terms[s + 1], spread, s) for s in range(n - 1)]
     gradient = pl.pallas_call(
         functools.partial(total_kernel, n),
         out_shape=struct(held, F32),

time: 35.1 us -> 33.4 us (0.952)
  waiting for transfers between devices: 15 us -> 13.1 us
    ppermute x6, waiting for transfers between devices: 12.5 us -> 10.7 us  [sent(): return lax.ppermute(x, ('snd', 'pt'), pairs)]
where the time goes in v4:
time: 33.4 us; the launch traced here: 33.2 us
  starting transfers between devices  13.4 us (40%)
  waiting for transfers between devices  13.1 us (39%)
  Pallas kernels  5.92 us (18%)
  local copies, waits for them, and re-layouts  0.7 us (2%)
    ppermute x6, starting transfers between devices, sent(): return lax.ppermute(x, ('snd', 'pt'), pairs)  11.8 us
    ppermute x6, waiting for transfers between devices, sent(): return lax.ppermute(x, ('snd', 'pt'), pairs)  10.7 us
    pallas_call x1, Pallas kernels, body(): pl.pallas_call(functools.partial(stage_kernel, gather, spread, tiles), ou...  2.64 us
    ppermute x1, waiting for transfers between devices, body(): other = lax.ppermute(mine, 'win', [(0, 1), (1, 0)])  2.42 us
    ppermute x1, starting transfers between devices, body(): other = lax.ppermute(mine, 'win', [(0, 1), (1, 0)])  1.56 us
    pallas_call x1, Pallas kernels, body(): pl.pallas_call(round_kernel, out_shape=struct(held, BF16), in_specs=[HBM]...  1 us
    pallas_call x1, Pallas kernels, body(): pl.pallas_call(functools.partial(total_kernel, n), out_shape=struct(held,...  0.81 us
    pallas_call x1, Pallas kernels, body(): pl.pallas_call(functools.partial(modeled_kernel, n), out_shape=struct((bl...  0.74 us
  transfers between devices with their start and end apart: 7, of which 4 were waited for; matrix products, arithmetic and copies ran while one was open for 0% of the time, Pallas kernels for 8%

profile of v4, /device:TPU:0, one launch (start us, length us, event | category | flops | bytes accessed | tf_op | source)
XLA Modules:
  0.0 33.2 jit_solution(11478691751748019037)
XLA Ops:
  0.0 1.0 %round.1.refs_0_ = bf16[64,8,128]{2,1,0:T(8,128)(2,1)S(1)} custom-call(f32[64,8,128]{2,1,0:T(8,128)} %bitcast.3), custom_call_target="tpu_custom_call" | custom-call | tf_op jit(solution)/shard_map/round/pallas_call | solution.py:140
  1.0 5.1 %collective-permute-start.2 = (bf16[64,8,128]{2,1,0:T(8,128)(2,1)S(1)}, bf16[64,8,128]{2,1,0:T(8,128)(2,1)S(1)}, u32[]{:S(2)}, u32[]{:S(2)}) collective-permute-start(bf16[64,8,128]{2,1,0:T(8,128)(2,1)S(1)} %round.1.refs_0_), channel_id=1, source_target_pairs={{0,12},{4,0},{8,4},{12,8},{1,5},{5,13},{9,1},{13,9},{2,14},{6,2},{... | collective-permute-start | bytes 393224 | tf_op jit(solution)/shard_map/ppermute | solution.py:34
  6.1 0.0 collective-permute-start.1
  6.1 1.0 %collective-permute-start = (bf16[64,8,128]{2,1,0:T(8,128)(2,1)S(1)}, bf16[64,8,128]{2,1,0:T(8,128)(2,1)S(1)}, u32[]{:S(2)}, u32[]{:S(2)}) collective-permute-start(bf16[64,8,128]{2,1,0:T(8,128)(2,1)S(1)} %round.1.refs_0_), channel_id=1, source_target_pairs={{0,4},{4,8},{8,12},{12,0},{1,9},{5,1},{9,13},{13,5},{2,6},{6,10},{... | collective-permute-start | bytes 393224 | tf_op jit(solution)/shard_map/ppermute | solution.py:34
  7.1 0.7 %copy-done.2 = s32[8,16]{1,0:T(8,128)S(1)} copy-done((s32[8,16]{1,0:T(8,128)S(1)}, s32[8,16]{1,0:T(8,128)}, u32[]{:S(2)}) %copy-start.2) | copy-done | bytes 536
  7.8 2.6 %stage.1 = (s32[8,16]{1,0:T(8,128)S(1)}, s32[8,16]{1,0:T(8,128)S(1)}, bf16[8,16,128,128]{3,2,1,0:T(8,128)(2,1)S(1)}, bf16[8,16,128,128]{3,2,1,0:T(8,128)(2,1)S(1)}) custom-call(s32[8,16]{1,0:T(8,128)S(1)} %copy-done.2, bf16[8,16,128,128]{3,2,1,0:T(8,128)(2,1)} %foot_ref.1), custom_call_target="tpu_custom_call" | custom-call | bytes 8388608 | tf_op jit(solution)/shard_map/stage/pallas_call | solution.py:151
  10.5 0.0 collective-permute-done.2.refs_3_
  10.5 6.6 %collective-permute-done.1.refs_2_ = bf16[64,8,128]{2,1,0:T(8,128)(2,1)S(1)} collective-permute-done((bf16[64,8,128]{2,1,0:T(8,128)(2,1)S(1)}, bf16[64,8,128]{2,1,0:T(8,128)(2,1)S(1)}, u32[]{:S(2)}, u32[]{:S(2)}) %collective-permute-start.1) | collective-permute-done | bytes 131104 | tf_op jit(solution)/shard_map/ppermute | solution.py:34
  17.1 0.0 collective-permute-done.refs_1_
  17.1 0.7 %modeled.1.mine_ref = f32[8,8,128]{2,1,0:T(8,128)S(1)} custom-call(s32[8,16]{1,0:T(8,128)S(1)} %get-tuple-element.14.take_ref, bf16[8,16,128,128]{3,2,1,0:T(8,128)(2,1)S(1)} %get-tuple-element.15.turned_ref, bf16[64,8,128]{2,1,0:T(8,128)(2,1)S(1)} %round.1.refs_0_, bf16[64,8,128]{2,1,0:T(8,128)(2,1)S(1)} %collective-permute-done.refs_1_, ...), custom_call_target="tpu_custom_call" | custom-call | tf_op jit(solution)/shard_map/modeled/pallas_call | solution.py:161
  17.8 1.6 %collective-permute-start.3 = (f32[8,8,128]{2,1,0:T(8,128)S(1)}, f32[8,8,128]{2,1,0:T(8,128)S(1)}, u32[]{:S(2)}, u32[]{:S(2)}) collective-permute-start(f32[8,8,128]{2,1,0:T(8,128)S(1)} %modeled.1.mine_ref), channel_id=1, source_target_pairs={{0,2},{2,0},{1,3},{3,1},{4,6},{6,4},{5,7},{7,5},{8,10},{10,8},{9,1... | collective-permute-start | bytes 98312 | tf_op jit(solution)/shard_map/ppermute | solution.py:171
  19.4 2.4 %collective-permute-done.3.other_ref = f32[8,8,128]{2,1,0:T(8,128)S(1)} collective-permute-done((f32[8,8,128]{2,1,0:T(8,128)S(1)}, f32[8,8,128]{2,1,0:T(8,128)S(1)}, u32[]{:S(2)}, u32[]{:S(2)}) %collective-permute-start.3) | collective-permute-done | bytes 32800 | tf_op jit(solution)/shard_map/ppermute | solution.py:171
  21.8 0.0 copy-done.3
  21.8 0.0 copy-done.4
  21.8 0.7 %terms.1 = (f32[64,8,128]{2,1,0:T(8,128)S(1)}, bf16[64,8,128]{2,1,0:T(8,128)(2,1)S(1)}, bf16[64,8,128]{2,1,0:T(8,128)(2,1)S(1)}, bf16[64,8,128]{2,1,0:T(8,128)(2,1)S(1)}) custom-call(s32[8,16]{1,0:T(8,128)S(1)} %get-tuple-element.13.put_ref, f32[8,8,128]{2,1,0:T(8,128)S(1)} %modeled.1.mine_ref, f32[8,8,128]{2,1,0:T(8,128)S(1)} %collective-permute-done.3.other_ref, ...), custom_call_target="tpu_custom_call" | custom-call | tf_op jit(solution)/shard_map/terms/pallas_call | solution.py:174
  22.6 0.9 %collective-permute-start.4 = (bf16[64,8,128]{2,1,0:T(8,128)(2,1)S(1)}, bf16[64,8,128]{2,1,0:T(8,128)(2,1)S(1)}, u32[]{:S(2)}, u32[]{:S(2)}) collective-permute-start(bf16[64,8,128]{2,1,0:T(8,128)(2,1)S(1)} %get-tuple-element.18), channel_id=1, source_target_pairs={{0,4},{4,8},{8,12},{12,0},{1,13},{5,9},{9,5},{13,1},{2,6},{6,10},{... | collective-permute-start | bytes 393224 | tf_op jit(solution)/shard_map/ppermute | solution.py:34
  23.4 2.0 %collective-permute-start.5 = (bf16[64,8,128]{2,1,0:T(8,128)(2,1)S(1)}, bf16[64,8,128]{2,1,0:T(8,128)(2,1)S(1)}, u32[]{:S(2)}, u32[]{:S(2)}) collective-permute-start(bf16[64,8,128]{2,1,0:T(8,128)(2,1)S(1)} %get-tuple-element.19), channel_id=1, source_target_pairs={{0,8},{4,12},{8,0},{12,4},{1,5},{5,13},{9,1},{13,9},{2,10},{6,14},... | collective-permute-start | bytes 393224 | tf_op jit(solution)/shard_map/ppermute | solution.py:34
  25.4 2.9 %collective-permute-start.6 = (bf16[64,8,128]{2,1,0:T(8,128)(2,1)S(1)}, bf16[64,8,128]{2,1,0:T(8,128)(2,1)S(1)}, u32[]{:S(2)}, u32[]{:S(2)}) collective-permute-start(bf16[64,8,128]{2,1,0:T(8,128)(2,1)S(1)} %get-tuple-element.20), channel_id=1, source_target_pairs={{0,12},{4,0},{8,4},{12,8},{1,9},{5,1},{9,13},{13,5},{2,14},{6,2},{... | collective-permute-start | bytes 393224 | tf_op jit(solution)/shard_map/ppermute | solution.py:34
  28.3 1.3 %collective-permute-done.4.refs_0_ = bf16[64,8,128]{2,1,0:T(8,128)(2,1)S(1)} collective-permute-done((bf16[64,8,128]{2,1,0:T(8,128)(2,1)S(1)}, bf16[64,8,128]{2,1,0:T(8,128)(2,1)S(1)}, u32[]{:S(2)}, u32[]{:S(2)}) %collective-permute-start.4) | collective-permute-done | bytes 131104 | tf_op jit(solution)/shard_map/ppermute | solution.py:34
  29.6 2.8 %collective-permute-done.5.refs_1_ = bf16[64,8,128]{2,1,0:T(8,128)(2,1)S(1)} collective-permute-done((bf16[64,8,128]{2,1,0:T(8,128)(2,1)S(1)}, bf16[64,8,128]{2,1,0:T(8,128)(2,1)S(1)}, u32[]{:S(2)}, u32[]{:S(2)}) %collective-permute-start.5) | collective-permute-done | bytes 131104 | tf_op jit(solution)/shard_map/ppermute | solution.py:34
  32.4 0.0 collective-permute-done.6.refs_2_
  32.4 0.0 copy-done
  32.4 0.0 copy-done.1
  32.4 0.8 %total.1 = f32[64,8,128]{2,1,0:T(8,128)} custom-call(f32[64,8,128]{2,1,0:T(8,128)S(1)} %bitcast.4, f32[64,128]{1,0:T(8,128)S(1)} %bitcast.5, f32[64,8,128]{2,1,0:T(8,128)S(1)} %get-tuple-element.17.own_ref, bf16[64,8,128]{2,1,0:T(8,128)(2,1)S(1)} %collective-permute-done.4.refs_0_, bf16[64,8,128]{2,1,0:T(8,128)(2,1)S(1)} %collective-permute-done.5.refs_1_, ...), custom_call_target="tpu_custom_call" | custom-call | tf_op jit(solution)/shard_map/total/pallas_call | solution.py:184
  (5 shorter events, 0.0 us)
Async XLA Ops:
  0.0 21.8 %copy-start.3 = (f32[8,128]{1,0:T(8,128)S(1)}, f32[8,128]{1,0:T(8,128)}, u32[]{:S(2)}) copy-start(f32[8,128]{1,0:T(8,128)} %obs_ref.1) | copy-start | bytes 12292
  0.0 21.8 %copy-start.4 = (f32[8,128]{1,0:T(8,128)S(1)}, f32[8,128]{1,0:T(8,128)}, u32[]{:S(2)}) copy-start(f32[8,128]{1,0:T(8,128)} %weight_ref.1) | copy-start | bytes 12292
  1.0 9.4 %collective-permute-start.2 = (bf16[64,8,128]{2,1,0:T(8,128)(2,1)S(1)}, bf16[64,8,128]{2,1,0:T(8,128)(2,1)S(1)}, u32[]{:S(2)}, u32[]{:S(2)}) collective-permute-start(bf16[64,8,128]{2,1,0:T(8,128)(2,1)S(1)} %round.1.refs_0_), channel_id=1, source_target_pairs={{0,12},{4,0},{8,4},{12,8},{1,5},{5,13},{9,1},{13,9},{2,14},{6,2},{... | collective-permute-start | bytes 393224 | tf_op jit(solution)/shard_map/ppermute | solution.py:34
  6.1 11.0 %collective-permute-start.1 = (bf16[64,8,128]{2,1,0:T(8,128)(2,1)S(1)}, bf16[64,8,128]{2,1,0:T(8,128)(2,1)S(1)}, u32[]{:S(2)}, u32[]{:S(2)}) collective-permute-start(bf16[64,8,128]{2,1,0:T(8,128)(2,1)S(1)} %round.1.refs_0_), channel_id=1, source_target_pairs={{0,8},{4,12},{8,0},{12,4},{1,13},{5,9},{9,5},{13,1},{2,10},{6,14},... | collective-permute-start | bytes 393224 | tf_op jit(solution)/shard_map/ppermute | solution.py:34
  6.1 11.0 %collective-permute-start = (bf16[64,8,128]{2,1,0:T(8,128)(2,1)S(1)}, bf16[64,8,128]{2,1,0:T(8,128)(2,1)S(1)}, u32[]{:S(2)}, u32[]{:S(2)}) collective-permute-start(bf16[64,8,128]{2,1,0:T(8,128)(2,1)S(1)} %round.1.refs_0_), channel_id=1, source_target_pairs={{0,4},{4,8},{8,12},{12,0},{1,9},{5,1},{9,13},{13,5},{2,6},{6,10},{... | collective-permute-start | bytes 393224 | tf_op jit(solution)/shard_map/ppermute | solution.py:34
  7.1 0.7 %copy-start.2 = (s32[8,16]{1,0:T(8,128)S(1)}, s32[8,16]{1,0:T(8,128)}, u32[]{:S(2)}) copy-start(s32[8,16]{1,0:T(8,128)} %ids_ref.1) | copy-start | bytes 1540
  17.1 15.3 %copy-start = (f32[1,64,8,128]{3,2,1,0:T(8,128)S(1)}, f32[1,64,8,128]{3,2,1,0:T(8,128)}, u32[]{:S(2)}) copy-start(f32[1,64,8,128]{3,2,1,0:T(8,128)} %param.6) | copy-start | bytes 786436
  17.1 15.3 %copy-start.1 = (f32[1,64,128]{2,1,0:T(8,128)S(1)}, f32[1,64,128]{2,1,0:T(8,128)}, u32[]{:S(2)}) copy-start(f32[1,64,128]{2,1,0:T(8,128)} %param.7) | copy-start | bytes 98308
  17.8 4.0 %collective-permute-start.3 = (f32[8,8,128]{2,1,0:T(8,128)S(1)}, f32[8,8,128]{2,1,0:T(8,128)S(1)}, u32[]{:S(2)}, u32[]{:S(2)}) collective-permute-start(f32[8,8,128]{2,1,0:T(8,128)S(1)} %modeled.1.mine_ref), channel_id=1, source_target_pairs={{0,2},{2,0},{1,3},{3,1},{4,6},{6,4},{5,7},{7,5},{8,10},{10,8},{9,1... | collective-permute-start | bytes 98312 | tf_op jit(solution)/shard_map/ppermute | solution.py:171
  22.6 7.0 %collective-permute-start.4 = (bf16[64,8,128]{2,1,0:T(8,128)(2,1)S(1)}, bf16[64,8,128]{2,1,0:T(8,128)(2,1)S(1)}, u32[]{:S(2)}, u32[]{:S(2)}) collective-permute-start(bf16[64,8,128]{2,1,0:T(8,128)(2,1)S(1)} %get-tuple-element.18), channel_id=1, source_target_pairs={{0,4},{4,8},{8,12},{12,0},{1,13},{5,9},{9,5},{13,1},{2,6},{6,10},{... | collective-permute-start | bytes 393224 | tf_op jit(solution)/shard_map/ppermute | solution.py:34
  23.4 8.9 %collective-permute-start.5 = (bf16[64,8,128]{2,1,0:T(8,128)(2,1)S(1)}, bf16[64,8,128]{2,1,0:T(8,128)(2,1)S(1)}, u32[]{:S(2)}, u32[]{:S(2)}) collective-permute-start(bf16[64,8,128]{2,1,0:T(8,128)(2,1)S(1)} %get-tuple-element.19), channel_id=1, source_target_pairs={{0,8},{4,12},{8,0},{12,4},{1,5},{5,13},{9,1},{13,9},{2,10},{6,14},... | collective-permute-start | bytes 393224 | tf_op jit(solution)/shard_map/ppermute | solution.py:34
  25.4 7.0 %collective-permute-start.6 = (bf16[64,8,128]{2,1,0:T(8,128)(2,1)S(1)}, bf16[64,8,128]{2,1,0:T(8,128)(2,1)S(1)}, u32[]{:S(2)}, u32[]{:S(2)}) collective-permute-start(bf16[64,8,128]{2,1,0:T(8,128)(2,1)S(1)} %get-tuple-element.20), channel_id=1, source_target_pairs={{0,12},{4,0},{8,4},{12,8},{1,9},{5,1},{9,13},{13,5},{2,14},{6,2},{... | collective-permute-start | bytes 393224 | tf_op jit(solution)/shard_map/ppermute | solution.py:34

commit v5 on v4

--- a/solution.py
+++ b/solution.py
@@ -12,8 +12,7 @@
 I32 = jnp.int32
 HBM = pl.BlockSpec(memory_space=pltpu.HBM)
 VMEM = pl.BlockSpec(memory_space=pltpu.VMEM)
-PARAMS = pltpu.CompilerParams(vmem_limit_bytes=40 << 20)
-PIECES = 4
+PARAMS = pltpu.CompilerParams(vmem_limit_bytes=24 << 20)
 
 
 NEXT, ACROSS, LAST = (1, 2, 3, 0), (2, 3, 0, 1), (3, 0, 1, 2)
@@ -23,7 +22,7 @@
 def plans(n, cores):
     if n == 4 and cores == 2:
         shifts = (NEXT, ACROSS, LAST)
-        return (shifts, (CYCLE, MIRROR, BACK)), (shifts, (MIRROR, BACK, CYCLE))
+        return ((CYCLE, MIRROR, BACK),) * cores, (shifts, (MIRROR, BACK, CYCLE))
     shifts = tuple(tuple((i + s) % n for i in range(n)) for s in range(1, n))
     return (shifts,) * cores, (shifts,) * cores
 
@@ -60,25 +59,15 @@
     return pltpu.with_memory_space_constraint(x, pltpu.HBM)
 
 
-def round_kernel(flux_ref, out_ref, buf_ref, sems):
-    size = flux_ref.shape[0] // PIECES
-    pieces = [pl.ds(i * size, size) for i in range(PIECES)]
-    copies = [
-        pltpu.make_async_copy(flux_ref.at[at], buf_ref.at[at], sems.at[i]) for i, at in enumerate(pieces)
-    ]
-    for copy in copies:
-        copy.start()
-    for copy, at in zip(copies, pieces):
-        copy.wait()
-        out_ref[at] = buf_ref[at].astype(BF16)
-
-
-def stage_kernel(gather, spread, tiles, ids_ref, foot_ref, take_ref, put_ref, foot_out, turned_ref, sems):
-    blocks, depth = ids_ref.shape
+def stage(gather, spread, tiles, ids_ref, foot_ref, take_ref, put_ref, foot_out, turned_ref, sems):
+    blocks = ids_ref.shape[0]
+    first = pltpu.make_async_copy(ids_ref, take_ref, sems.at[blocks])
+    first.start()
     copies = [pltpu.make_async_copy(foot_ref.at[b], foot_out.at[b], sems.at[b]) for b in range(blocks)]
     for copy in copies:
         copy.start()
-    ids = ids_ref[...]
+    first.wait()
+    ids = take_ref[...]
     shift = tiles.bit_length() - 1
     owner = lax.shift_right_logical(ids, shift)
     local = ids - lax.shift_left(owner, shift)
@@ -87,6 +76,35 @@
     for b in range(blocks):
         copies[b].wait()
         turned_ref[b] = jnp.swapaxes(foot_out[b], 1, 2)
+
+
+def first_kernel(gather, spread, tiles, flux_ref, ids_ref, foot_ref, rounded_ref, *refs):
+    staged, (buf_ref, flux_sem, sems) = refs[:4], refs[4:]
+    copy = pltpu.make_async_copy(flux_ref, buf_ref, flux_sem)
+    copy.start()
+
+    @pl.when(lax.axis_index("pt") == 0)
+    def _():
+        stage(gather, spread, tiles, ids_ref, foot_ref, *staged, sems)
+
+    copy.wait()
+    rounded_ref[...] = buf_ref[...].astype(BF16)
+
+
+def second_kernel(gather, spread, tiles, ids_ref, foot_ref, *refs):
+    early, late, (sems,) = refs[:4], refs[4:8], refs[8:]
+
+    @pl.when(lax.axis_index("pt") != 0)
+    def _():
+        stage(gather, spread, tiles, ids_ref, foot_ref, *late, sems)
+
+    @pl.when(lax.axis_index("pt") == 0)
+    def _():
+        copies = [pltpu.make_async_copy(a, b, sems.at[i]) for i, (a, b) in enumerate(zip(early, late))]
+        for copy in copies:
+            copy.start()
+        for copy in copies:
+            copy.wait()
 
 
 def modeled_kernel(n, take_ref, turned_ref, *refs):
@@ -134,30 +152,36 @@
     flux = flux_state[0]
     tiles, points, cells = flux.shape
     blocks, depth, soundings, _ = footprint.shape
-    assert tiles & (tiles - 1) == 0 and tiles % PIECES == 0
+    assert tiles & (tiles - 1) == 0
     held = (tiles, points, cells)
 
-    rounded = pl.pallas_call(
-        round_kernel,
-        out_shape=struct(held, BF16),
-        in_specs=[HBM],
-        out_specs=VMEM,
-        scratch_shapes=[pltpu.VMEM(held, F32), pltpu.SemaphoreType.DMA((PIECES,))],
-        compiler_params=PARAMS,
-        name="round",
-    )(in_hbm(flux))
     gather, spread = plans(n, lax.axis_size("pt"))
+    staged = [struct(tile_ids.shape, I32)] * 2 + [struct(footprint.shape, BF16)] * 2
+    raw = in_hbm(tile_ids), in_hbm(footprint)
+    rounded, *early = pl.pallas_call(
+        functools.partial(first_kernel, gather, spread, tiles),
+        out_shape=[struct(held, BF16)] + staged,
+        in_specs=[HBM] * 3,
+        out_specs=[VMEM] * 5,
+        scratch_shapes=[
+            pltpu.VMEM(held, F32),
+            pltpu.SemaphoreType.DMA,
+            pltpu.SemaphoreType.DMA((blocks + 1,)),
+        ],
+        compiler_params=PARAMS,
+        name="first",
+    )(in_hbm(flux), *raw)
     shards = [rounded] + [sent(rounded, gather, s) for s in range(n - 1)]
     take, put, foot, turned = pl.pallas_call(
-        functools.partial(stage_kernel, gather, spread, tiles),
-        out_shape=[struct(tile_ids.shape, I32)] * 2 + [struct(footprint.shape, BF16)] * 2,
-        in_specs=[VMEM, HBM],
+        functools.partial(second_kernel, gather, spread, tiles),
+        out_shape=staged,
+        in_specs=[HBM] * 2 + [VMEM] * 4,
         out_specs=[VMEM] * 4,
-        scratch_shapes=[pltpu.SemaphoreType.DMA((blocks,))],
+        scratch_shapes=[pltpu.SemaphoreType.DMA((blocks + 1,))],
         compiler_params=PARAMS,
         cost_estimate=pl.CostEstimate(flops=0, transcendentals=0, bytes_accessed=footprint.size * 4),
-        name="stage",
-    )(tile_ids, in_hbm(footprint))
+        name="second",
+    )(*raw, *early)
     mine = pl.pallas_call(
         functools.partial(modeled_kernel, n),
         out_shape=struct((blocks, points, soundings), F32),

time: 33.4 us -> 32.9 us (0.985)
  starting transfers between devices: 13.4 us -> 14.7 us
  waiting for transfers between devices: 13.1 us -> 12.2 us
  local copies, waits for them, and re-layouts: 0.7 us -> 0.02 us
    ppermute x6, starting transfers between devices: 11.8 us -> 13.2 us  [sent(): return lax.ppermute(x, ('snd', 'pt'), pairs)]
    ppermute x6, waiting for transfers between devices: 10.7 us -> 9.78 us  [sent(): return lax.ppermute(x, ('snd', 'pt'), pairs)]
    unnamed x10 -> x8, local copies, waits for them, and re-layouts: 0.7 us -> 0.02 us
  transfers between devices with their start and end apart: 7 -> 7, of which waited for: 4 -> 4; matrix products, arithmetic and copies ran while one was open for 0% -> 0% of each run, Pallas kernels for 8% -> 2%
where the time goes in v5:
time: 32.9 us; the launch traced here: 32.7 us
  starting transfers between devices  14.7 us (45%)
  waiting for transfers between devices  12.2 us (37%)
  Pallas kernels  5.7 us (17%)
    ppermute x6, starting transfers between devices, sent(): return lax.ppermute(x, ('snd', 'pt'), pairs)  13.2 us
    ppermute x6, waiting for transfers between devices, sent(): return lax.ppermute(x, ('snd', 'pt'), pairs)  9.78 us
    pallas_call x1, Pallas kernels, body(): pl.pallas_call(functools.partial(first_kernel, gather, spread, tiles), ou...  2.77 us
    ppermute x1, waiting for transfers between devices, body(): other = lax.ppermute(mine, 'win', [(0, 1), (1, 0)])  2.41 us
    ppermute x1, starting transfers between devices, body(): other = lax.ppermute(mine, 'win', [(0, 1), (1, 0)])  1.57 us
    pallas_call x1, Pallas kernels, body(): pl.pallas_call(functools.partial(total_kernel, n), out_shape=struct(held,...  0.81 us
    pallas_call x1, Pallas kernels, body(): pl.pallas_call(functools.partial(modeled_kernel, n), out_shape=struct((bl...  0.74 us
    pallas_call x1, Pallas kernels, body(): pl.pallas_call(functools.partial(terms_kernel, n), out_shape=[struct(held...  0.73 us
  transfers between devices with their start and end apart: 7, of which 4 were waited for; matrix products, arithmetic and copies ran while one was open for 0% of the time, Pallas kernels for 2%

profile of v5, /device:TPU:0, one launch (start us, length us, event | category | flops | bytes accessed | tf_op | source)
XLA Modules:
  0.0 32.7 jit_solution(3467012155944245058)
XLA Ops:
  0.0 2.8 %first.1 = (bf16[64,8,128]{2,1,0:T(8,128)(2,1)S(1)}, s32[8,16]{1,0:T(8,128)S(1)}, s32[8,16]{1,0:T(8,128)S(1)}, bf16[8,16,128,128]{3,2,1,0:T(8,128)(2,1)S(1)}, bf16[8,16,128,128]{3,2,1,0:T(8,128)(2,1)S(1)}) custom-call(f32[64,8,128]{2,1,0:T(8,128)} %bitcast.3, s32[8,16]{1,0:T(8,128)} %ids_ref.3, bf16[8,16,128,128]{3,2,1,0:T(8,128)(2,1)} %foot_ref.3), custom_call_target="tpu_custom_call" | custom-call | tf_op jit(solution)/shard_map/first/pallas_call | solution.py:161
  2.8 3.1 %collective-permute-start.2 = (bf16[64,8,128]{2,1,0:T(8,128)(2,1)S(1)}, bf16[64,8,128]{2,1,0:T(8,128)(2,1)S(1)}, u32[]{:S(2)}, u32[]{:S(2)}) collective-permute-start(bf16[64,8,128]{2,1,0:T(8,128)(2,1)S(1)} %get-tuple-element.25.refs_0_), channel_id=1, source_target_pairs={{0,4},{4,12},{8,0},{12,8},{1,5},{5,13},{9,1},{13,9},{2,6},{6,14},{... | collective-permute-start | bytes 393224 | tf_op jit(solution)/shard_map/ppermute | solution.py:33
  5.9 2.5 %collective-permute-start.1 = (bf16[64,8,128]{2,1,0:T(8,128)(2,1)S(1)}, bf16[64,8,128]{2,1,0:T(8,128)(2,1)S(1)}, u32[]{:S(2)}, u32[]{:S(2)}) collective-permute-start(bf16[64,8,128]{2,1,0:T(8,128)(2,1)S(1)} %get-tuple-element.25.refs_0_), channel_id=1, source_target_pairs={{0,12},{4,8},{8,4},{12,0},{1,13},{5,9},{9,5},{13,1},{2,14},{6,10},... | collective-permute-start | bytes 393224 | tf_op jit(solution)/shard_map/ppermute | solution.py:33
  8.3 1.6 %collective-permute-start = (bf16[64,8,128]{2,1,0:T(8,128)(2,1)S(1)}, bf16[64,8,128]{2,1,0:T(8,128)(2,1)S(1)}, u32[]{:S(2)}, u32[]{:S(2)}) collective-permute-start(bf16[64,8,128]{2,1,0:T(8,128)(2,1)S(1)} %get-tuple-element.25.refs_0_), channel_id=1, source_target_pairs={{0,8},{4,0},{8,12},{12,4},{1,9},{5,1},{9,13},{13,5},{2,10},{6,2},{... | collective-permute-start | bytes 393224 | tf_op jit(solution)/shard_map/ppermute | solution.py:33
  9.9 0.6 %second.1 = (s32[8,16]{1,0:T(8,128)S(1)}, s32[8,16]{1,0:T(8,128)S(1)}, bf16[8,16,128,128]{3,2,1,0:T(8,128)(2,1)S(1)}, bf16[8,16,128,128]{3,2,1,0:T(8,128)(2,1)S(1)}) custom-call(s32[8,16]{1,0:T(8,128)} %ids_ref.3, bf16[8,16,128,128]{3,2,1,0:T(8,128)(2,1)} %foot_ref.3, s32[8,16]{1,0:T(8,128)S(1)} %get-tuple-element.18.refs_0_, ...), custom_call_target="tpu_custom_call" | custom-call | bytes 8388608 | tf_op jit(solution)/shard_map/second/pallas_call | solution.py:175
  10.6 0.0 copy-start.2
  10.6 0.0 copy-start.3
  10.6 6.2 %collective-permute-done.2.refs_3_ = bf16[64,8,128]{2,1,0:T(8,128)(2,1)S(1)} collective-permute-done((bf16[64,8,128]{2,1,0:T(8,128)(2,1)S(1)}, bf16[64,8,128]{2,1,0:T(8,128)(2,1)S(1)}, u32[]{:S(2)}, u32[]{:S(2)}) %collective-permute-start.2) | collective-permute-done | bytes 131104 | tf_op jit(solution)/shard_map/ppermute | solution.py:33
  16.8 0.0 collective-permute-done.1.refs_2_
  16.8 0.0 collective-permute-done.refs_1_
  16.8 0.0 copy-start.1
  16.8 0.7 %modeled.1.mine_ref = f32[8,8,128]{2,1,0:T(8,128)S(1)} custom-call(s32[8,16]{1,0:T(8,128)S(1)} %get-tuple-element.23.take_ref, bf16[8,16,128,128]{3,2,1,0:T(8,128)(2,1)S(1)} %get-tuple-element.24.turned_ref, bf16[64,8,128]{2,1,0:T(8,128)(2,1)S(1)} %get-tuple-element.25.refs_0_, bf16[64,8,128]{2,1,0:T(8,128)(2,1)S(1)} %collective-permute-done.refs_1_, ...), custom_call_target="tpu_custom_call" | custom-call | tf_op jit(solution)/shard_map/modeled/pallas_call | solution.py:185
  17.6 1.6 %collective-permute-start.3 = (f32[8,8,128]{2,1,0:T(8,128)S(1)}, f32[8,8,128]{2,1,0:T(8,128)S(1)}, u32[]{:S(2)}, u32[]{:S(2)}) collective-permute-start(f32[8,8,128]{2,1,0:T(8,128)S(1)} %modeled.1.mine_ref), channel_id=1, source_target_pairs={{0,2},{2,0},{1,3},{3,1},{4,6},{6,4},{5,7},{7,5},{8,10},{10,8},{9,1... | collective-permute-start | bytes 98312 | tf_op jit(solution)/shard_map/ppermute | solution.py:195
  19.1 2.4 %collective-permute-done.3.other_ref = f32[8,8,128]{2,1,0:T(8,128)S(1)} collective-permute-done((f32[8,8,128]{2,1,0:T(8,128)S(1)}, f32[8,8,128]{2,1,0:T(8,128)S(1)}, u32[]{:S(2)}, u32[]{:S(2)}) %collective-permute-start.3) | collective-permute-done | bytes 32800 | tf_op jit(solution)/shard_map/ppermute | solution.py:195
  21.5 0.0 copy-done.2
  21.5 0.0 copy-done.3
  21.5 0.7 %terms.1 = (f32[64,8,128]{2,1,0:T(8,128)S(1)}, bf16[64,8,128]{2,1,0:T(8,128)(2,1)S(1)}, bf16[64,8,128]{2,1,0:T(8,128)(2,1)S(1)}, bf16[64,8,128]{2,1,0:T(8,128)(2,1)S(1)}) custom-call(s32[8,16]{1,0:T(8,128)S(1)} %get-tuple-element.22.put_ref, f32[8,8,128]{2,1,0:T(8,128)S(1)} %modeled.1.mine_ref, f32[8,8,128]{2,1,0:T(8,128)S(1)} %collective-permute-done.3.other_ref, ...), custom_call_target="tpu_custom_call" | custom-call | tf_op jit(solution)/shard_map/terms/pallas_call | solution.py:198
  22.3 2.0 %collective-permute-start.4 = (bf16[64,8,128]{2,1,0:T(8,128)(2,1)S(1)}, bf16[64,8,128]{2,1,0:T(8,128)(2,1)S(1)}, u32[]{:S(2)}, u32[]{:S(2)}) collective-permute-start(bf16[64,8,128]{2,1,0:T(8,128)(2,1)S(1)} %get-tuple-element.28), channel_id=1, source_target_pairs={{0,4},{4,8},{8,12},{12,0},{1,13},{5,9},{9,5},{13,1},{2,6},{6,10},{... | collective-permute-start | bytes 393224 | tf_op jit(solution)/shard_map/ppermute | solution.py:33
  24.3 1.2 %collective-permute-start.5 = (bf16[64,8,128]{2,1,0:T(8,128)(2,1)S(1)}, bf16[64,8,128]{2,1,0:T(8,128)(2,1)S(1)}, u32[]{:S(2)}, u32[]{:S(2)}) collective-permute-start(bf16[64,8,128]{2,1,0:T(8,128)(2,1)S(1)} %get-tuple-element.29), channel_id=1, source_target_pairs={{0,8},{4,12},{8,0},{12,4},{1,5},{5,13},{9,1},{13,9},{2,10},{6,14},... | collective-permute-start | bytes 393224 | tf_op jit(solution)/shard_map/ppermute | solution.py:33
  25.5 2.9 %collective-permute-start.6 = (bf16[64,8,128]{2,1,0:T(8,128)(2,1)S(1)}, bf16[64,8,128]{2,1,0:T(8,128)(2,1)S(1)}, u32[]{:S(2)}, u32[]{:S(2)}) collective-permute-start(bf16[64,8,128]{2,1,0:T(8,128)(2,1)S(1)} %get-tuple-element.30), channel_id=1, source_target_pairs={{0,12},{4,0},{8,4},{12,8},{1,9},{5,1},{9,13},{13,5},{2,14},{6,2},{... | collective-permute-start | bytes 393224 | tf_op jit(solution)/shard_map/ppermute | solution.py:33
  28.3 0.8 %collective-permute-done.4.refs_0_ = bf16[64,8,128]{2,1,0:T(8,128)(2,1)S(1)} collective-permute-done((bf16[64,8,128]{2,1,0:T(8,128)(2,1)S(1)}, bf16[64,8,128]{2,1,0:T(8,128)(2,1)S(1)}, u32[]{:S(2)}, u32[]{:S(2)}) %collective-permute-start.4) | collective-permute-done | bytes 131104 | tf_op jit(solution)/shard_map/ppermute | solution.py:33
  29.1 2.8 %collective-permute-done.5.refs_1_ = bf16[64,8,128]{2,1,0:T(8,128)(2,1)S(1)} collective-permute-done((bf16[64,8,128]{2,1,0:T(8,128)(2,1)S(1)}, bf16[64,8,128]{2,1,0:T(8,128)(2,1)S(1)}, u32[]{:S(2)}, u32[]{:S(2)}) %collective-permute-start.5) | collective-permute-done | bytes 131104 | tf_op jit(solution)/shard_map/ppermute | solution.py:33
  31.9 0.0 collective-permute-done.6.refs_2_
  31.9 0.8 %total.1 = f32[64,8,128]{2,1,0:T(8,128)} custom-call(f32[64,8,128]{2,1,0:T(8,128)S(1)} %bitcast.4, f32[64,128]{1,0:T(8,128)S(1)} %bitcast.5, f32[64,8,128]{2,1,0:T(8,128)S(1)} %get-tuple-element.27.own_ref, bf16[64,8,128]{2,1,0:T(8,128)(2,1)S(1)} %collective-permute-done.4.refs_0_, bf16[64,8,128]{2,1,0:T(8,128)(2,1)S(1)} %collective-permute-done.5.refs_1_, ...), custom_call_target="tpu_custom_call" | custom-call | tf_op jit(solution)/shard_map/total/pallas_call | solution.py:208
  (3 shorter events, 0.0 us)
Async XLA Ops:
  2.8 14.0 %collective-permute-start.2 = (bf16[64,8,128]{2,1,0:T(8,128)(2,1)S(1)}, bf16[64,8,128]{2,1,0:T(8,128)(2,1)S(1)}, u32[]{:S(2)}, u32[]{:S(2)}) collective-permute-start(bf16[64,8,128]{2,1,0:T(8,128)(2,1)S(1)} %get-tuple-element.25.refs_0_), channel_id=1, source_target_pairs={{0,4},{4,12},{8,0},{12,8},{1,5},{5,13},{9,1},{13,9},{2,6},{6,14},{... | collective-permute-start | bytes 393224 | tf_op jit(solution)/shard_map/ppermute | solution.py:33
  5.9 10.9 %collective-permute-start.1 = (bf16[64,8,128]{2,1,0:T(8,128)(2,1)S(1)}, bf16[64,8,128]{2,1,0:T(8,128)(2,1)S(1)}, u32[]{:S(2)}, u32[]{:S(2)}) collective-permute-start(bf16[64,8,128]{2,1,0:T(8,128)(2,1)S(1)} %get-tuple-element.25.refs_0_), channel_id=1, source_target_pairs={{0,12},{4,8},{8,4},{12,0},{1,13},{5,9},{9,5},{13,1},{2,14},{6,10},... | collective-permute-start | bytes 393224 | tf_op jit(solution)/shard_map/ppermute | solution.py:33
  8.3 8.5 %collective-permute-start = (bf16[64,8,128]{2,1,0:T(8,128)(2,1)S(1)}, bf16[64,8,128]{2,1,0:T(8,128)(2,1)S(1)}, u32[]{:S(2)}, u32[]{:S(2)}) collective-permute-start(bf16[64,8,128]{2,1,0:T(8,128)(2,1)S(1)} %get-tuple-element.25.refs_0_), channel_id=1, source_target_pairs={{0,8},{4,0},{8,12},{12,4},{1,9},{5,1},{9,13},{13,5},{2,10},{6,2},{... | collective-permute-start | bytes 393224 | tf_op jit(solution)/shard_map/ppermute | solution.py:33
  10.6 11.0 %copy-start.2 = (f32[8,128]{1,0:T(8,128)S(1)}, f32[8,128]{1,0:T(8,128)}, u32[]{:S(2)}) copy-start(f32[8,128]{1,0:T(8,128)} %obs_ref.1) | copy-start | bytes 12292
  10.6 11.0 %copy-start.3 = (f32[8,128]{1,0:T(8,128)S(1)}, f32[8,128]{1,0:T(8,128)}, u32[]{:S(2)}) copy-start(f32[8,128]{1,0:T(8,128)} %weight_ref.1) | copy-start | bytes 12292
  16.8 15.1 %copy-start = (f32[1,64,8,128]{3,2,1,0:T(8,128)S(1)}, f32[1,64,8,128]{3,2,1,0:T(8,128)}, u32[]{:S(2)}) copy-start(f32[1,64,8,128]{3,2,1,0:T(8,128)} %param.6) | copy-start | bytes 786436
  16.8 15.1 %copy-start.1 = (f32[1,64,128]{2,1,0:T(8,128)S(1)}, f32[1,64,128]{2,1,0:T(8,128)}, u32[]{:S(2)}) copy-start(f32[1,64,128]{2,1,0:T(8,128)} %param.7) | copy-start | bytes 98308
  17.6 4.0 %collective-permute-start.3 = (f32[8,8,128]{2,1,0:T(8,128)S(1)}, f32[8,8,128]{2,1,0:T(8,128)S(1)}, u32[]{:S(2)}, u32[]{:S(2)}) collective-permute-start(f32[8,8,128]{2,1,0:T(8,128)S(1)} %modeled.1.mine_ref), channel_id=1, source_target_pairs={{0,2},{2,0},{1,3},{3,1},{4,6},{6,4},{5,7},{7,5},{8,10},{10,8},{9,1... | collective-permute-start | bytes 98312 | tf_op jit(solution)/shard_map/ppermute | solution.py:195
  22.3 6.8 %collective-permute-start.4 = (bf16[64,8,128]{2,1,0:T(8,128)(2,1)S(1)}, bf16[64,8,128]{2,1,0:T(8,128)(2,1)S(1)}, u32[]{:S(2)}, u32[]{:S(2)}) collective-permute-start(bf16[64,8,128]{2,1,0:T(8,128)(2,1)S(1)} %get-tuple-element.28), channel_id=1, source_target_pairs={{0,4},{4,8},{8,12},{12,0},{1,13},{5,9},{9,5},{13,1},{2,6},{6,10},{... | collective-permute-start | bytes 393224 | tf_op jit(solution)/shard_map/ppermute | solution.py:33
  24.3 7.6 %collective-permute-start.5 = (bf16[64,8,128]{2,1,0:T(8,128)(2,1)S(1)}, bf16[64,8,128]{2,1,0:T(8,128)(2,1)S(1)}, u32[]{:S(2)}, u32[]{:S(2)}) collective-permute-start(bf16[64,8,128]{2,1,0:T(8,128)(2,1)S(1)} %get-tuple-element.29), channel_id=1, source_target_pairs={{0,8},{4,12},{8,0},{12,4},{1,5},{5,13},{9,1},{13,9},{2,10},{6,14},... | collective-permute-start | bytes 393224 | tf_op jit(solution)/shard_map/ppermute | solution.py:33
  25.5 6.4 %collective-permute-start.6 = (bf16[64,8,128]{2,1,0:T(8,128)(2,1)S(1)}, bf16[64,8,128]{2,1,0:T(8,128)(2,1)S(1)}, u32[]{:S(2)}, u32[]{:S(2)}) collective-permute-start(bf16[64,8,128]{2,1,0:T(8,128)(2,1)S(1)} %get-tuple-element.30), channel_id=1, source_target_pairs={{0,12},{4,0},{8,4},{12,8},{1,9},{5,1},{9,13},{13,5},{2,14},{6,2},{... | collective-permute-start | bytes 393224 | tf_op jit(solution)/shard_map/ppermute | solution.py:33

commit v6 on v5

--- a/solution.py
+++ b/solution.py
@@ -138,9 +138,13 @@
         outs[slot][...] = dense_ref[pl.ds(slot * tiles, tiles)].astype(outs[slot].dtype)
 
 
-def total_kernel(n, flux_ref, prior_ref, own_ref, *refs):
+def base_kernel(flux_ref, prior_ref, own_ref, out_ref):
+    out_ref[...] = own_ref[...] + prior_ref[...][:, None, :] * flux_ref[...]
+
+
+def total_kernel(n, base_ref, *refs):
     arrived, out_ref = refs[: n - 1], refs[n - 1]
-    total = own_ref[...] + prior_ref[...][:, None, :] * flux_ref[...]
+    total = base_ref[...]
     for a in arrived:
         total += a[...].astype(F32)
     out_ref[...] = total
@@ -205,14 +209,23 @@
         name="terms",
     )(put, mine, other, observed, obs_weight, foot)
     arrived = [sent(terms[s + 1], spread, s) for s in range(n - 1)]
+    base = pl.pallas_call(
+        base_kernel,
+        out_shape=struct(held, F32),
+        in_specs=[VMEM] * 3,
+        out_specs=VMEM,
+        compiler_params=PARAMS,
+        cost_estimate=pl.CostEstimate(flops=0, transcendentals=0, bytes_accessed=footprint.size),
+        name="base",
+    )(flux, prior_precision[0], terms[0])
     gradient = pl.pallas_call(
         functools.partial(total_kernel, n),
         out_shape=struct(held, F32),
-        in_specs=[VMEM] * (n + 2),
+        in_specs=[VMEM] * n,
         out_specs=VMEM,
         compiler_params=PARAMS,
         name="total",
-    )(flux, prior_precision[0], terms[0], *arrived)
+    )(base, *arrived)
     return gradient[None]
 
 

time: 32.9 us -> 32.8 us (level)
  no operation moved by 1% of the time
where the time goes in v6:
time: 32.8 us; the launch traced here: 32.7 us
  starting transfers between devices  14.7 us (45%)
  waiting for transfers between devices  12.1 us (37%)
  Pallas kernels  5.7 us (17%)
    ppermute x6, starting transfers between devices, sent(): return lax.ppermute(x, ('snd', 'pt'), pairs)  13.2 us
    ppermute x6, waiting for transfers between devices, sent(): return lax.ppermute(x, ('snd', 'pt'), pairs)  9.72 us
    pallas_call x1, Pallas kernels, body(): pl.pallas_call(functools.partial(first_kernel, gather, spread, tiles), ou...  2.77 us
    ppermute x1, waiting for transfers between devices, body(): other = lax.ppermute(mine, 'win', [(0, 1), (1, 0)])  2.42 us
    ppermute x1, starting transfers between devices, body(): other = lax.ppermute(mine, 'win', [(0, 1), (1, 0)])  1.56 us
    pallas_call x1, Pallas kernels, body(): pl.pallas_call(functools.partial(total_kernel, n), out_shape=struct(held,...  0.76 us
    pallas_call x1, Pallas kernels, body(): pl.pallas_call(functools.partial(modeled_kernel, n), out_shape=struct((bl...  0.74 us
    pallas_call x1, Pallas kernels, body(): pl.pallas_call(functools.partial(terms_kernel, n), out_shape=[struct(held...  0.74 us
  transfers between devices with their start and end apart: 7, of which 4 were waited for; matrix products, arithmetic and copies ran while one was open for 0% of the time, Pallas kernels for 2%

profile of v6, /device:TPU:0, one launch (start us, length us, event | category | flops | bytes accessed | tf_op | source)
XLA Modules:
  0.0 32.7 jit_solution(14156408464279149710)
XLA Ops:
  0.0 2.8 %first.1 = (bf16[64,8,128]{2,1,0:T(8,128)(2,1)S(1)}, s32[8,16]{1,0:T(8,128)S(1)}, s32[8,16]{1,0:T(8,128)S(1)}, bf16[8,16,128,128]{3,2,1,0:T(8,128)(2,1)S(1)}, bf16[8,16,128,128]{3,2,1,0:T(8,128)(2,1)S(1)}) custom-call(f32[64,8,128]{2,1,0:T(8,128)} %bitcast.3, s32[8,16]{1,0:T(8,128)} %ids_ref.3, bf16[8,16,128,128]{3,2,1,0:T(8,128)(2,1)} %foot_ref.3), custom_call_target="tpu_custom_call" | custom-call | tf_op jit(solution)/shard_map/first/pallas_call | solution.py:165
  2.8 3.1 %collective-permute-start.2 = (bf16[64,8,128]{2,1,0:T(8,128)(2,1)S(1)}, bf16[64,8,128]{2,1,0:T(8,128)(2,1)S(1)}, u32[]{:S(2)}, u32[]{:S(2)}) collective-permute-start(bf16[64,8,128]{2,1,0:T(8,128)(2,1)S(1)} %get-tuple-element.25.refs_0_), channel_id=1, source_target_pairs={{0,4},{4,12},{8,0},{12,8},{1,5},{5,13},{9,1},{13,9},{2,6},{6,14},{... | collective-permute-start | bytes 393224 | tf_op jit(solution)/shard_map/ppermute | solution.py:33
  5.9 2.5 %collective-permute-start.1 = (bf16[64,8,128]{2,1,0:T(8,128)(2,1)S(1)}, bf16[64,8,128]{2,1,0:T(8,128)(2,1)S(1)}, u32[]{:S(2)}, u32[]{:S(2)}) collective-permute-start(bf16[64,8,128]{2,1,0:T(8,128)(2,1)S(1)} %get-tuple-element.25.refs_0_), channel_id=1, source_target_pairs={{0,12},{4,8},{8,4},{12,0},{1,13},{5,9},{9,5},{13,1},{2,14},{6,10},... | collective-permute-start | bytes 393224 | tf_op jit(solution)/shard_map/ppermute | solution.py:33
  8.3 1.6 %collective-permute-start = (bf16[64,8,128]{2,1,0:T(8,128)(2,1)S(1)}, bf16[64,8,128]{2,1,0:T(8,128)(2,1)S(1)}, u32[]{:S(2)}, u32[]{:S(2)}) collective-permute-start(bf16[64,8,128]{2,1,0:T(8,128)(2,1)S(1)} %get-tuple-element.25.refs_0_), channel_id=1, source_target_pairs={{0,8},{4,0},{8,12},{12,4},{1,9},{5,1},{9,13},{13,5},{2,10},{6,2},{... | collective-permute-start | bytes 393224 | tf_op jit(solution)/shard_map/ppermute | solution.py:33
  9.9 0.6 %second.1 = (s32[8,16]{1,0:T(8,128)S(1)}, s32[8,16]{1,0:T(8,128)S(1)}, bf16[8,16,128,128]{3,2,1,0:T(8,128)(2,1)S(1)}, bf16[8,16,128,128]{3,2,1,0:T(8,128)(2,1)S(1)}) custom-call(s32[8,16]{1,0:T(8,128)} %ids_ref.3, bf16[8,16,128,128]{3,2,1,0:T(8,128)(2,1)} %foot_ref.3, s32[8,16]{1,0:T(8,128)S(1)} %get-tuple-element.18.refs_0_, ...), custom_call_target="tpu_custom_call" | custom-call | bytes 8388608 | tf_op jit(solution)/shard_map/second/pallas_call | solution.py:179
  10.6 0.0 copy-start.2
  10.6 0.0 copy-start.3
  10.6 6.2 %collective-permute-done.2.refs_3_ = bf16[64,8,128]{2,1,0:T(8,128)(2,1)S(1)} collective-permute-done((bf16[64,8,128]{2,1,0:T(8,128)(2,1)S(1)}, bf16[64,8,128]{2,1,0:T(8,128)(2,1)S(1)}, u32[]{:S(2)}, u32[]{:S(2)}) %collective-permute-start.2) | collective-permute-done | bytes 131104 | tf_op jit(solution)/shard_map/ppermute | solution.py:33
  16.8 0.0 collective-permute-done.1.refs_2_
  16.8 0.0 collective-permute-done.refs_1_
  16.8 0.0 copy-start.1
  16.8 0.7 %modeled.1.mine_ref = f32[8,8,128]{2,1,0:T(8,128)S(1)} custom-call(s32[8,16]{1,0:T(8,128)S(1)} %get-tuple-element.23.take_ref, bf16[8,16,128,128]{3,2,1,0:T(8,128)(2,1)S(1)} %get-tuple-element.24.turned_ref, bf16[64,8,128]{2,1,0:T(8,128)(2,1)S(1)} %get-tuple-element.25.refs_0_, bf16[64,8,128]{2,1,0:T(8,128)(2,1)S(1)} %collective-permute-done.refs_1_, ...), custom_call_target="tpu_custom_call" | custom-call | tf_op jit(solution)/shard_map/modeled/pallas_call | solution.py:189
  17.6 1.6 %collective-permute-start.3 = (f32[8,8,128]{2,1,0:T(8,128)S(1)}, f32[8,8,128]{2,1,0:T(8,128)S(1)}, u32[]{:S(2)}, u32[]{:S(2)}) collective-permute-start(f32[8,8,128]{2,1,0:T(8,128)S(1)} %modeled.1.mine_ref), channel_id=1, source_target_pairs={{0,2},{2,0},{1,3},{3,1},{4,6},{6,4},{5,7},{7,5},{8,10},{10,8},{9,1... | collective-permute-start | bytes 98312 | tf_op jit(solution)/shard_map/ppermute | solution.py:199
  19.1 2.4 %collective-permute-done.3.other_ref = f32[8,8,128]{2,1,0:T(8,128)S(1)} collective-permute-done((f32[8,8,128]{2,1,0:T(8,128)S(1)}, f32[8,8,128]{2,1,0:T(8,128)S(1)}, u32[]{:S(2)}, u32[]{:S(2)}) %collective-permute-start.3) | collective-permute-done | bytes 32800 | tf_op jit(solution)/shard_map/ppermute | solution.py:199
  21.5 0.0 copy-done.2
  21.5 0.7 %terms.1 = (f32[64,8,128]{2,1,0:T(8,128)S(1)}, bf16[64,8,128]{2,1,0:T(8,128)(2,1)S(1)}, bf16[64,8,128]{2,1,0:T(8,128)(2,1)S(1)}, bf16[64,8,128]{2,1,0:T(8,128)(2,1)S(1)}) custom-call(s32[8,16]{1,0:T(8,128)S(1)} %get-tuple-element.22.put_ref, f32[8,8,128]{2,1,0:T(8,128)S(1)} %modeled.1.mine_ref, f32[8,8,128]{2,1,0:T(8,128)S(1)} %collective-permute-done.3.other_ref, ...), custom_call_target="tpu_custom_call" | custom-call | tf_op jit(solution)/shard_map/terms/pallas_call | solution.py:202
  22.3 2.0 %collective-permute-start.4 = (bf16[64,8,128]{2,1,0:T(8,128)(2,1)S(1)}, bf16[64,8,128]{2,1,0:T(8,128)(2,1)S(1)}, u32[]{:S(2)}, u32[]{:S(2)}) collective-permute-start(bf16[64,8,128]{2,1,0:T(8,128)(2,1)S(1)} %get-tuple-element.28), channel_id=1, source_target_pairs={{0,4},{4,8},{8,12},{12,0},{1,13},{5,9},{9,5},{13,1},{2,6},{6,10},{... | collective-permute-start | bytes 393224 | tf_op jit(solution)/shard_map/ppermute | solution.py:33
  24.3 1.2 %collective-permute-start.5 = (bf16[64,8,128]{2,1,0:T(8,128)(2,1)S(1)}, bf16[64,8,128]{2,1,0:T(8,128)(2,1)S(1)}, u32[]{:S(2)}, u32[]{:S(2)}) collective-permute-start(bf16[64,8,128]{2,1,0:T(8,128)(2,1)S(1)} %get-tuple-element.29), channel_id=1, source_target_pairs={{0,8},{4,12},{8,0},{12,4},{1,5},{5,13},{9,1},{13,9},{2,10},{6,14},... | collective-permute-start | bytes 393224 | tf_op jit(solution)/shard_map/ppermute | solution.py:33
  25.5 2.8 %collective-permute-start.6 = (bf16[64,8,128]{2,1,0:T(8,128)(2,1)S(1)}, bf16[64,8,128]{2,1,0:T(8,128)(2,1)S(1)}, u32[]{:S(2)}, u32[]{:S(2)}) collective-permute-start(bf16[64,8,128]{2,1,0:T(8,128)(2,1)S(1)} %get-tuple-element.30), channel_id=1, source_target_pairs={{0,12},{4,0},{8,4},{12,8},{1,9},{5,1},{9,13},{13,5},{2,14},{6,2},{... | collective-permute-start | bytes 393224 | tf_op jit(solution)/shard_map/ppermute | solution.py:33
  28.3 0.0 copy-done.1
  28.4 0.7 %collective-permute-done.4.refs_0_ = bf16[64,8,128]{2,1,0:T(8,128)(2,1)S(1)} collective-permute-done((bf16[64,8,128]{2,1,0:T(8,128)(2,1)S(1)}, bf16[64,8,128]{2,1,0:T(8,128)(2,1)S(1)}, u32[]{:S(2)}, u32[]{:S(2)}) %collective-permute-start.4) | collective-permute-done | bytes 131104 | tf_op jit(solution)/shard_map/ppermute | solution.py:33
  29.1 2.8 %collective-permute-done.5.refs_1_ = bf16[64,8,128]{2,1,0:T(8,128)(2,1)S(1)} collective-permute-done((bf16[64,8,128]{2,1,0:T(8,128)(2,1)S(1)}, bf16[64,8,128]{2,1,0:T(8,128)(2,1)S(1)}, u32[]{:S(2)}, u32[]{:S(2)}) %collective-permute-start.5) | collective-permute-done | bytes 131104 | tf_op jit(solution)/shard_map/ppermute | solution.py:33
  31.9 0.0 collective-permute-done.6.refs_2_
  31.9 0.8 %total.1 = f32[64,8,128]{2,1,0:T(8,128)} custom-call(f32[64,8,128]{2,1,0:T(8,128)S(1)} %base.1.base_ref, bf16[64,8,128]{2,1,0:T(8,128)(2,1)S(1)} %collective-permute-done.4.refs_0_, bf16[64,8,128]{2,1,0:T(8,128)(2,1)S(1)} %collective-permute-done.5.refs_1_, bf16[64,8,128]{2,1,0:T(8,128)(2,1)S(1)} %collective-permute-done.6.refs_2_), custom_call_target="tpu_custom_call" | custom-call | tf_op jit(solution)/shard_map/total/pallas_call | solution.py:221
  (4 shorter events, 0.1 us)
Async XLA Ops:
  2.8 14.0 %collective-permute-start.2 = (bf16[64,8,128]{2,1,0:T(8,128)(2,1)S(1)}, bf16[64,8,128]{2,1,0:T(8,128)(2,1)S(1)}, u32[]{:S(2)}, u32[]{:S(2)}) collective-permute-start(bf16[64,8,128]{2,1,0:T(8,128)(2,1)S(1)} %get-tuple-element.25.refs_0_), channel_id=1, source_target_pairs={{0,4},{4,12},{8,0},{12,8},{1,5},{5,13},{9,1},{13,9},{2,6},{6,14},{... | collective-permute-start | bytes 393224 | tf_op jit(solution)/shard_map/ppermute | solution.py:33
  5.9 10.9 %collective-permute-start.1 = (bf16[64,8,128]{2,1,0:T(8,128)(2,1)S(1)}, bf16[64,8,128]{2,1,0:T(8,128)(2,1)S(1)}, u32[]{:S(2)}, u32[]{:S(2)}) collective-permute-start(bf16[64,8,128]{2,1,0:T(8,128)(2,1)S(1)} %get-tuple-element.25.refs_0_), channel_id=1, source_target_pairs={{0,12},{4,8},{8,4},{12,0},{1,13},{5,9},{9,5},{13,1},{2,14},{6,10},... | collective-permute-start | bytes 393224 | tf_op jit(solution)/shard_map/ppermute | solution.py:33
  8.3 8.5 %collective-permute-start = (bf16[64,8,128]{2,1,0:T(8,128)(2,1)S(1)}, bf16[64,8,128]{2,1,0:T(8,128)(2,1)S(1)}, u32[]{:S(2)}, u32[]{:S(2)}) collective-permute-start(bf16[64,8,128]{2,1,0:T(8,128)(2,1)S(1)} %get-tuple-element.25.refs_0_), channel_id=1, source_target_pairs={{0,8},{4,0},{8,12},{12,4},{1,9},{5,1},{9,13},{13,5},{2,10},{6,2},{... | collective-permute-start | bytes 393224 | tf_op jit(solution)/shard_map/ppermute | solution.py:33
  10.6 11.0 %copy-start.2 = (f32[8,128]{1,0:T(8,128)S(1)}, f32[8,128]{1,0:T(8,128)}, u32[]{:S(2)}) copy-start(f32[8,128]{1,0:T(8,128)} %obs_ref.1) | copy-start | bytes 12292
  10.6 11.0 %copy-start.3 = (f32[8,128]{1,0:T(8,128)S(1)}, f32[8,128]{1,0:T(8,128)}, u32[]{:S(2)}) copy-start(f32[8,128]{1,0:T(8,128)} %weight_ref.1) | copy-start | bytes 12292
  16.8 11.6 %copy-start = (f32[1,64,8,128]{3,2,1,0:T(8,128)S(1)}, f32[1,64,8,128]{3,2,1,0:T(8,128)}, u32[]{:S(2)}) copy-start(f32[1,64,8,128]{3,2,1,0:T(8,128)} %param.6) | copy-start | bytes 786436
  16.8 11.6 %copy-start.1 = (f32[1,64,128]{2,1,0:T(8,128)S(1)}, f32[1,64,128]{2,1,0:T(8,128)}, u32[]{:S(2)}) copy-start(f32[1,64,128]{2,1,0:T(8,128)} %param.7) | copy-start | bytes 98308
  17.6 4.0 %collective-permute-start.3 = (f32[8,8,128]{2,1,0:T(8,128)S(1)}, f32[8,8,128]{2,1,0:T(8,128)S(1)}, u32[]{:S(2)}, u32[]{:S(2)}) collective-permute-start(f32[8,8,128]{2,1,0:T(8,128)S(1)} %modeled.1.mine_ref), channel_id=1, source_target_pairs={{0,2},{2,0},{1,3},{3,1},{4,6},{6,4},{5,7},{7,5},{8,10},{10,8},{9,1... | collective-permute-start | bytes 98312 | tf_op jit(solution)/shard_map/ppermute | solution.py:199
  22.3 6.8 %collective-permute-start.4 = (bf16[64,8,128]{2,1,0:T(8,128)(2,1)S(1)}, bf16[64,8,128]{2,1,0:T(8,128)(2,1)S(1)}, u32[]{:S(2)}, u32[]{:S(2)}) collective-permute-start(bf16[64,8,128]{2,1,0:T(8,128)(2,1)S(1)} %get-tuple-element.28), channel_id=1, source_target_pairs={{0,4},{4,8},{8,12},{12,0},{1,13},{5,9},{9,5},{13,1},{2,6},{6,10},{... | collective-permute-start | bytes 393224 | tf_op jit(solution)/shard_map/ppermute | solution.py:33
  24.3 7.6 %collective-permute-start.5 = (bf16[64,8,128]{2,1,0:T(8,128)(2,1)S(1)}, bf16[64,8,128]{2,1,0:T(8,128)(2,1)S(1)}, u32[]{:S(2)}, u32[]{:S(2)}) collective-permute-start(bf16[64,8,128]{2,1,0:T(8,128)(2,1)S(1)} %get-tuple-element.29), channel_id=1, source_target_pairs={{0,8},{4,12},{8,0},{12,4},{1,5},{5,13},{9,1},{13,9},{2,10},{6,14},... | collective-permute-start | bytes 393224 | tf_op jit(solution)/shard_map/ppermute | solution.py:33
  25.5 6.4 %collective-permute-start.6 = (bf16[64,8,128]{2,1,0:T(8,128)(2,1)S(1)}, bf16[64,8,128]{2,1,0:T(8,128)(2,1)S(1)}, u32[]{:S(2)}, u32[]{:S(2)}) collective-permute-start(bf16[64,8,128]{2,1,0:T(8,128)(2,1)S(1)} %get-tuple-element.30), channel_id=1, source_target_pairs={{0,12},{4,0},{8,4},{12,8},{1,9},{5,1},{9,13},{13,5},{2,14},{6,2},{... | collective-permute-start | bytes 393224 | tf_op jit(solution)/shard_map/ppermute | solution.py:33

commit v7 on v6

--- a/solution.py
+++ b/solution.py
@@ -143,11 +143,19 @@
 
 
 def total_kernel(n, base_ref, *refs):
-    arrived, out_ref = refs[: n - 1], refs[n - 1]
-    total = base_ref[...]
-    for a in arrived:
-        total += a[...].astype(F32)
-    out_ref[...] = total
+    arrived, (out_ref, sum_ref, sems) = refs[: n - 1], refs[n - 1 :]
+    size = sum_ref.shape[0] // 2
+    copies = []
+    for i in range(2):
+        at = pl.ds(i * size, size)
+        total = base_ref[at]
+        for a in arrived:
+            total += a[at].astype(F32)
+        sum_ref[at] = total
+        copies.append(pltpu.make_async_copy(sum_ref.at[at], out_ref.at[at], sems.at[i]))
+        copies[i].start()
+    for copy in copies:
+        copy.wait()
 
 
 def body(flux_state, prior_precision, footprint, tile_ids, observed, obs_weight):
@@ -222,7 +230,8 @@
         functools.partial(total_kernel, n),
         out_shape=struct(held, F32),
         in_specs=[VMEM] * n,
-        out_specs=VMEM,
+        out_specs=HBM,
+        scratch_shapes=[pltpu.VMEM(held, F32), pltpu.SemaphoreType.DMA((2,))],
         compiler_params=PARAMS,
         name="total",
     )(base, *arrived)

time: 32.8 us -> 32.8 us (level)
  no operation moved by 1% of the time
where the time goes in v7:
time: 32.8 us; the launch traced here: 32.7 us
  starting transfers between devices  14.7 us (45%)
  waiting for transfers between devices  12.1 us (37%)
  Pallas kernels  5.68 us (17%)
    ppermute x6, starting transfers between devices, sent(): return lax.ppermute(x, ('snd', 'pt'), pairs)  13.2 us
    ppermute x6, waiting for transfers between devices, sent(): return lax.ppermute(x, ('snd', 'pt'), pairs)  9.73 us
    pallas_call x1, Pallas kernels, body(): pl.pallas_call(functools.partial(first_kernel, gather, spread, tiles), ou...  2.77 us
    ppermute x1, waiting for transfers between devices, body(): other = lax.ppermute(mine, 'win', [(0, 1), (1, 0)])  2.42 us
    ppermute x1, starting transfers between devices, body(): other = lax.ppermute(mine, 'win', [(0, 1), (1, 0)])  1.56 us
    pallas_call x1, Pallas kernels, body(): pl.pallas_call(functools.partial(total_kernel, n), out_shape=struct(held,...  0.74 us
    pallas_call x1, Pallas kernels, body(): pl.pallas_call(functools.partial(modeled_kernel, n), out_shape=struct((bl...  0.74 us
    pallas_call x1, Pallas kernels, body(): pl.pallas_call(functools.partial(terms_kernel, n), out_shape=[struct(held...  0.74 us
  transfers between devices with their start and end apart: 7, of which 4 were waited for; matrix products, arithmetic and copies ran while one was open for 0% of the time, Pallas kernels for 2%

profile of v7, /device:TPU:0, one launch (start us, length us, event | category | flops | bytes accessed | tf_op | source)
XLA Modules:
  0.0 32.7 jit_solution(5247635647625105912)
XLA Ops:
  0.0 2.8 %first.1 = (bf16[64,8,128]{2,1,0:T(8,128)(2,1)S(1)}, s32[8,16]{1,0:T(8,128)S(1)}, s32[8,16]{1,0:T(8,128)S(1)}, bf16[8,16,128,128]{3,2,1,0:T(8,128)(2,1)S(1)}, bf16[8,16,128,128]{3,2,1,0:T(8,128)(2,1)S(1)}) custom-call(f32[64,8,128]{2,1,0:T(8,128)} %bitcast.3, s32[8,16]{1,0:T(8,128)} %ids_ref.3, bf16[8,16,128,128]{3,2,1,0:T(8,128)(2,1)} %foot_ref.3), custom_call_target="tpu_custom_call" | custom-call | tf_op jit(solution)/shard_map/first/pallas_call | solution.py:173
  2.8 3.1 %collective-permute-start.2 = (bf16[64,8,128]{2,1,0:T(8,128)(2,1)S(1)}, bf16[64,8,128]{2,1,0:T(8,128)(2,1)S(1)}, u32[]{:S(2)}, u32[]{:S(2)}) collective-permute-start(bf16[64,8,128]{2,1,0:T(8,128)(2,1)S(1)} %get-tuple-element.25.refs_0_), channel_id=1, source_target_pairs={{0,4},{4,12},{8,0},{12,8},{1,5},{5,13},{9,1},{13,9},{2,6},{6,14},{... | collective-permute-start | bytes 393224 | tf_op jit(solution)/shard_map/ppermute | solution.py:33
  5.9 2.5 %collective-permute-start.1 = (bf16[64,8,128]{2,1,0:T(8,128)(2,1)S(1)}, bf16[64,8,128]{2,1,0:T(8,128)(2,1)S(1)}, u32[]{:S(2)}, u32[]{:S(2)}) collective-permute-start(bf16[64,8,128]{2,1,0:T(8,128)(2,1)S(1)} %get-tuple-element.25.refs_0_), channel_id=1, source_target_pairs={{0,12},{4,8},{8,4},{12,0},{1,13},{5,9},{9,5},{13,1},{2,14},{6,10},... | collective-permute-start | bytes 393224 | tf_op jit(solution)/shard_map/ppermute | solution.py:33
  8.3 1.6 %collective-permute-start = (bf16[64,8,128]{2,1,0:T(8,128)(2,1)S(1)}, bf16[64,8,128]{2,1,0:T(8,128)(2,1)S(1)}, u32[]{:S(2)}, u32[]{:S(2)}) collective-permute-start(bf16[64,8,128]{2,1,0:T(8,128)(2,1)S(1)} %get-tuple-element.25.refs_0_), channel_id=1, source_target_pairs={{0,8},{4,0},{8,12},{12,4},{1,9},{5,1},{9,13},{13,5},{2,10},{6,2},{... | collective-permute-start | bytes 393224 | tf_op jit(solution)/shard_map/ppermute | solution.py:33
  9.9 0.6 %second.1 = (s32[8,16]{1,0:T(8,128)S(1)}, s32[8,16]{1,0:T(8,128)S(1)}, bf16[8,16,128,128]{3,2,1,0:T(8,128)(2,1)S(1)}, bf16[8,16,128,128]{3,2,1,0:T(8,128)(2,1)S(1)}) custom-call(s32[8,16]{1,0:T(8,128)} %ids_ref.3, bf16[8,16,128,128]{3,2,1,0:T(8,128)(2,1)} %foot_ref.3, s32[8,16]{1,0:T(8,128)S(1)} %get-tuple-element.18.refs_0_, ...), custom_call_target="tpu_custom_call" | custom-call | bytes 8388608 | tf_op jit(solution)/shard_map/second/pallas_call | solution.py:187
  10.6 0.0 copy-start.2
  10.6 0.0 copy-start.3
  10.6 6.2 %collective-permute-done.2.refs_3_ = bf16[64,8,128]{2,1,0:T(8,128)(2,1)S(1)} collective-permute-done((bf16[64,8,128]{2,1,0:T(8,128)(2,1)S(1)}, bf16[64,8,128]{2,1,0:T(8,128)(2,1)S(1)}, u32[]{:S(2)}, u32[]{:S(2)}) %collective-permute-start.2) | collective-permute-done | bytes 131104 | tf_op jit(solution)/shard_map/ppermute | solution.py:33
  16.8 0.0 collective-permute-done.1.refs_2_
  16.8 0.0 collective-permute-done.refs_1_
  16.8 0.0 copy-start.1
  16.8 0.7 %modeled.1.mine_ref = f32[8,8,128]{2,1,0:T(8,128)S(1)} custom-call(s32[8,16]{1,0:T(8,128)S(1)} %get-tuple-element.23.take_ref, bf16[8,16,128,128]{3,2,1,0:T(8,128)(2,1)S(1)} %get-tuple-element.24.turned_ref, bf16[64,8,128]{2,1,0:T(8,128)(2,1)S(1)} %get-tuple-element.25.refs_0_, bf16[64,8,128]{2,1,0:T(8,128)(2,1)S(1)} %collective-permute-done.refs_1_, ...), custom_call_target="tpu_custom_call" | custom-call | tf_op jit(solution)/shard_map/modeled/pallas_call | solution.py:197
  17.6 1.6 %collective-permute-start.3 = (f32[8,8,128]{2,1,0:T(8,128)S(1)}, f32[8,8,128]{2,1,0:T(8,128)S(1)}, u32[]{:S(2)}, u32[]{:S(2)}) collective-permute-start(f32[8,8,128]{2,1,0:T(8,128)S(1)} %modeled.1.mine_ref), channel_id=1, source_target_pairs={{0,2},{2,0},{1,3},{3,1},{4,6},{6,4},{5,7},{7,5},{8,10},{10,8},{9,1... | collective-permute-start | bytes 98312 | tf_op jit(solution)/shard_map/ppermute | solution.py:207
  19.1 2.4 %collective-permute-done.3.other_ref = f32[8,8,128]{2,1,0:T(8,128)S(1)} collective-permute-done((f32[8,8,128]{2,1,0:T(8,128)S(1)}, f32[8,8,128]{2,1,0:T(8,128)S(1)}, u32[]{:S(2)}, u32[]{:S(2)}) %collective-permute-start.3) | collective-permute-done | bytes 32800 | tf_op jit(solution)/shard_map/ppermute | solution.py:207
  21.5 0.0 copy-done.2
  21.5 0.0 copy-done.3
  21.5 0.7 %terms.1 = (f32[64,8,128]{2,1,0:T(8,128)S(1)}, bf16[64,8,128]{2,1,0:T(8,128)(2,1)S(1)}, bf16[64,8,128]{2,1,0:T(8,128)(2,1)S(1)}, bf16[64,8,128]{2,1,0:T(8,128)(2,1)S(1)}) custom-call(s32[8,16]{1,0:T(8,128)S(1)} %get-tuple-element.22.put_ref, f32[8,8,128]{2,1,0:T(8,128)S(1)} %modeled.1.mine_ref, f32[8,8,128]{2,1,0:T(8,128)S(1)} %collective-permute-done.3.other_ref, ...), custom_call_target="tpu_custom_call" | custom-call | tf_op jit(solution)/shard_map/terms/pallas_call | solution.py:210
  22.3 2.0 %collective-permute-start.4 = (bf16[64,8,128]{2,1,0:T(8,128)(2,1)S(1)}, bf16[64,8,128]{2,1,0:T(8,128)(2,1)S(1)}, u32[]{:S(2)}, u32[]{:S(2)}) collective-permute-start(bf16[64,8,128]{2,1,0:T(8,128)(2,1)S(1)} %get-tuple-element.28), channel_id=1, source_target_pairs={{0,4},{4,8},{8,12},{12,0},{1,13},{5,9},{9,5},{13,1},{2,6},{6,10},{... | collective-permute-start | bytes 393224 | tf_op jit(solution)/shard_map/ppermute | solution.py:33
  24.3 1.2 %collective-permute-start.5 = (bf16[64,8,128]{2,1,0:T(8,128)(2,1)S(1)}, bf16[64,8,128]{2,1,0:T(8,128)(2,1)S(1)}, u32[]{:S(2)}, u32[]{:S(2)}) collective-permute-start(bf16[64,8,128]{2,1,0:T(8,128)(2,1)S(1)} %get-tuple-element.29), channel_id=1, source_target_pairs={{0,8},{4,12},{8,0},{12,4},{1,5},{5,13},{9,1},{13,9},{2,10},{6,14},... | collective-permute-start | bytes 393224 | tf_op jit(solution)/shard_map/ppermute | solution.py:33
  25.5 2.8 %collective-permute-start.6 = (bf16[64,8,128]{2,1,0:T(8,128)(2,1)S(1)}, bf16[64,8,128]{2,1,0:T(8,128)(2,1)S(1)}, u32[]{:S(2)}, u32[]{:S(2)}) collective-permute-start(bf16[64,8,128]{2,1,0:T(8,128)(2,1)S(1)} %get-tuple-element.30), channel_id=1, source_target_pairs={{0,12},{4,0},{8,4},{12,8},{1,9},{5,1},{9,13},{13,5},{2,14},{6,2},{... | collective-permute-start | bytes 393224 | tf_op jit(solution)/shard_map/ppermute | solution.py:33
  28.4 0.7 %collective-permute-done.4.refs_0_ = bf16[64,8,128]{2,1,0:T(8,128)(2,1)S(1)} collective-permute-done((bf16[64,8,128]{2,1,0:T(8,128)(2,1)S(1)}, bf16[64,8,128]{2,1,0:T(8,128)(2,1)S(1)}, u32[]{:S(2)}, u32[]{:S(2)}) %collective-permute-start.4) | collective-permute-done | bytes 131104 | tf_op jit(solution)/shard_map/ppermute | solution.py:33
  29.1 2.8 %collective-permute-done.5.refs_1_ = bf16[64,8,128]{2,1,0:T(8,128)(2,1)S(1)} collective-permute-done((bf16[64,8,128]{2,1,0:T(8,128)(2,1)S(1)}, bf16[64,8,128]{2,1,0:T(8,128)(2,1)S(1)}, u32[]{:S(2)}, u32[]{:S(2)}) %collective-permute-start.5) | collective-permute-done | bytes 131104 | tf_op jit(solution)/shard_map/ppermute | solution.py:33
  31.9 0.0 collective-permute-done.6.refs_2_
  31.9 0.7 %total.1 = f32[64,8,128]{2,1,0:T(8,128)} custom-call(f32[64,8,128]{2,1,0:T(8,128)S(1)} %base.1.base_ref, bf16[64,8,128]{2,1,0:T(8,128)(2,1)S(1)} %collective-permute-done.4.refs_0_, bf16[64,8,128]{2,1,0:T(8,128)(2,1)S(1)} %collective-permute-done.5.refs_1_, bf16[64,8,128]{2,1,0:T(8,128)(2,1)S(1)} %collective-permute-done.6.refs_2_), custom_call_target="tpu_custom_call" | custom-call | tf_op jit(solution)/shard_map/total/pallas_call | solution.py:229
  (4 shorter events, 0.1 us)
Async XLA Ops:
  2.8 14.0 %collective-permute-start.2 = (bf16[64,8,128]{2,1,0:T(8,128)(2,1)S(1)}, bf16[64,8,128]{2,1,0:T(8,128)(2,1)S(1)}, u32[]{:S(2)}, u32[]{:S(2)}) collective-permute-start(bf16[64,8,128]{2,1,0:T(8,128)(2,1)S(1)} %get-tuple-element.25.refs_0_), channel_id=1, source_target_pairs={{0,4},{4,12},{8,0},{12,8},{1,5},{5,13},{9,1},{13,9},{2,6},{6,14},{... | collective-permute-start | bytes 393224 | tf_op jit(solution)/shard_map/ppermute | solution.py:33
  5.9 10.9 %collective-permute-start.1 = (bf16[64,8,128]{2,1,0:T(8,128)(2,1)S(1)}, bf16[64,8,128]{2,1,0:T(8,128)(2,1)S(1)}, u32[]{:S(2)}, u32[]{:S(2)}) collective-permute-start(bf16[64,8,128]{2,1,0:T(8,128)(2,1)S(1)} %get-tuple-element.25.refs_0_), channel_id=1, source_target_pairs={{0,12},{4,8},{8,4},{12,0},{1,13},{5,9},{9,5},{13,1},{2,14},{6,10},... | collective-permute-start | bytes 393224 | tf_op jit(solution)/shard_map/ppermute | solution.py:33
  8.3 8.5 %collective-permute-start = (bf16[64,8,128]{2,1,0:T(8,128)(2,1)S(1)}, bf16[64,8,128]{2,1,0:T(8,128)(2,1)S(1)}, u32[]{:S(2)}, u32[]{:S(2)}) collective-permute-start(bf16[64,8,128]{2,1,0:T(8,128)(2,1)S(1)} %get-tuple-element.25.refs_0_), channel_id=1, source_target_pairs={{0,8},{4,0},{8,12},{12,4},{1,9},{5,1},{9,13},{13,5},{2,10},{6,2},{... | collective-permute-start | bytes 393224 | tf_op jit(solution)/shard_map/ppermute | solution.py:33
  10.6 11.0 %copy-start.2 = (f32[8,128]{1,0:T(8,128)S(1)}, f32[8,128]{1,0:T(8,128)}, u32[]{:S(2)}) copy-start(f32[8,128]{1,0:T(8,128)} %obs_ref.1) | copy-start | bytes 12292
  10.6 11.0 %copy-start.3 = (f32[8,128]{1,0:T(8,128)S(1)}, f32[8,128]{1,0:T(8,128)}, u32[]{:S(2)}) copy-start(f32[8,128]{1,0:T(8,128)} %weight_ref.1) | copy-start | bytes 12292
  16.8 11.5 %copy-start = (f32[1,64,8,128]{3,2,1,0:T(8,128)S(1)}, f32[1,64,8,128]{3,2,1,0:T(8,128)}, u32[]{:S(2)}) copy-start(f32[1,64,8,128]{3,2,1,0:T(8,128)} %param.6) | copy-start | bytes 786436
  16.8 11.5 %copy-start.1 = (f32[1,64,128]{2,1,0:T(8,128)S(1)}, f32[1,64,128]{2,1,0:T(8,128)}, u32[]{:S(2)}) copy-start(f32[1,64,128]{2,1,0:T(8,128)} %param.7) | copy-start | bytes 98308
  17.6 4.0 %collective-permute-start.3 = (f32[8,8,128]{2,1,0:T(8,128)S(1)}, f32[8,8,128]{2,1,0:T(8,128)S(1)}, u32[]{:S(2)}, u32[]{:S(2)}) collective-permute-start(f32[8,8,128]{2,1,0:T(8,128)S(1)} %modeled.1.mine_ref), channel_id=1, source_target_pairs={{0,2},{2,0},{1,3},{3,1},{4,6},{6,4},{5,7},{7,5},{8,10},{10,8},{9,1... | collective-permute-start | bytes 98312 | tf_op jit(solution)/shard_map/ppermute | solution.py:207
  22.3 6.8 %collective-permute-start.4 = (bf16[64,8,128]{2,1,0:T(8,128)(2,1)S(1)}, bf16[64,8,128]{2,1,0:T(8,128)(2,1)S(1)}, u32[]{:S(2)}, u32[]{:S(2)}) collective-permute-start(bf16[64,8,128]{2,1,0:T(8,128)(2,1)S(1)} %get-tuple-element.28), channel_id=1, source_target_pairs={{0,4},{4,8},{8,12},{12,0},{1,13},{5,9},{9,5},{13,1},{2,6},{6,10},{... | collective-permute-start | bytes 393224 | tf_op jit(solution)/shard_map/ppermute | solution.py:33
  24.3 7.6 %collective-permute-start.5 = (bf16[64,8,128]{2,1,0:T(8,128)(2,1)S(1)}, bf16[64,8,128]{2,1,0:T(8,128)(2,1)S(1)}, u32[]{:S(2)}, u32[]{:S(2)}) collective-permute-start(bf16[64,8,128]{2,1,0:T(8,128)(2,1)S(1)} %get-tuple-element.29), channel_id=1, source_target_pairs={{0,8},{4,12},{8,0},{12,4},{1,5},{5,13},{9,1},{13,9},{2,10},{6,14},... | collective-permute-start | bytes 393224 | tf_op jit(solution)/shard_map/ppermute | solution.py:33
  25.5 6.4 %collective-permute-start.6 = (bf16[64,8,128]{2,1,0:T(8,128)(2,1)S(1)}, bf16[64,8,128]{2,1,0:T(8,128)(2,1)S(1)}, u32[]{:S(2)}, u32[]{:S(2)}) collective-permute-start(bf16[64,8,128]{2,1,0:T(8,128)(2,1)S(1)} %get-tuple-element.30), channel_id=1, source_target_pairs={{0,12},{4,0},{8,4},{12,8},{1,9},{5,1},{9,13},{13,5},{2,14},{6,2},{... | collective-permute-start | bytes 393224 | tf_op jit(solution)/shard_map/ppermute | solution.py:33
